TPU v7x, 32 devices: a whole 2x2x4 slice. The times are simulated.
32 devices in a mesh: ctx: 16 (over z, y, core), ch: 2 (over x).
Axes of the slice: x: 2, y: 2, z: 4, core: 2. Of those that a mesh axis runs over, the one named last changes fastest.
Arguments:
- query_proj: bfloat16 [2048, 8192], P('ctx', 'ch'), may hold values from -31 to 31
- key_proj: bfloat16 [2048, 8192], P('ctx', 'ch'), may hold values from -6 to 6
- value_proj: bfloat16 [2048, 8192], P('ctx', 'ch'), may hold values from -6 to 6
- key_taps: bfloat16 [512, 3], P('ch'), may hold values from -3.5 to 3.5
- value_taps: bfloat16 [512, 3], P('ch'), may hold values from -3.5 to 3.5
- residues: float32 [512, 16], P('ch'), may hold values from -0.06 to 0.06
- decay_rates: float32 [512, 16], P('ch'), may hold values from 5e-06 to 0.05
- skip_weight: float32 [8192], P('ch'), may hold values from 0.5 to 1.5
- norm_gain: float32 [8192], P('ch'), may hold values from 0.5 to 1.5
- out_grad: bfloat16 [2048, 8192], P('ctx', 'ch'), may hold values from -6 to 6
Outputs:
- mixed_out: bfloat16 [2048, 8192], P('ctx', 'ch')
- query_grad: bfloat16 [2048, 8192], P('ctx', 'ch')
- key_grad: bfloat16 [2048, 8192], P('ctx', 'ch')
- value_grad: bfloat16 [2048, 8192], P('ctx', 'ch')
- key_taps_grad: float32 [512, 3], P('ch')
- value_taps_grad: float32 [512, 3], P('ch')
- skip_grad: float32 [8192], P('ch')
- gain_grad: float32 [8192], P('ch')
All inputs are finite; a program needn't handle non-finite values.
Results may differ from a plain program's by a relative error of at most 0.006.
Values may be sent and summed in bfloat16 or wider, within the bound.
A program may use at most 128 MiB of HBM per device.

v0:
```python
import jax
import jax.numpy as jnp
from jax import lax
from jax.sharding import PartitionSpec as P

EPSILON = 1e-06
HIGHEST = lax.Precision.HIGHEST


def passed_along(value, axis, steps):
    count = lax.axis_size(axis)
    leading, last = (max(0, -steps), min(count, count - steps))
    return lax.ppermute(value, axis, [(source, source + steps) for source in range(leading, last)])


def short_apply(signal, tail_rows, spread):
    tok_rows = signal.shape[0]
    tap_count = spread.shape[1]
    extended = jnp.concatenate([tail_rows, signal], 0).astype(jnp.float32)
    accum = jnp.zeros(signal.shape, jnp.float32)
    for offset in range(tap_count):
        begin = tap_count - 1 - offset
        accum = accum + extended[begin : begin + tok_rows] * spread[:, offset][None, :]
    return (accum, extended)


def short_adjoint(grad_rows, head_rows, spread):
    tok_rows = grad_rows.shape[0]
    tap_count = spread.shape[1]
    extended = jnp.concatenate([grad_rows, head_rows], 0).astype(jnp.float32)
    accum = jnp.zeros(grad_rows.shape, jnp.float32)
    for offset in range(tap_count):
        accum = accum + extended[offset : offset + tok_rows] * spread[:, offset][None, :]
    return accum


def taps_gradient(grad_rows, extended, groups, tap_count):
    tok_rows, channels = grad_rows.shape
    grad_wide = grad_rows.astype(jnp.float32)
    columns = []
    for offset in range(tap_count):
        begin = tap_count - 1 - offset
        per_channel = jnp.sum(grad_wide * extended[begin : begin + tok_rows], axis=0)
        columns.append(jnp.sum(per_channel.reshape(groups, channels // groups), axis=1))
    return jnp.stack(columns, axis=1)


def local(
    query_proj,
    key_proj,
    value_proj,
    key_taps,
    value_taps,
    residues,
    decay_rates,
    skip_weight,
    norm_gain,
    out_grad,
):
    tok_rows, channels = key_proj.shape
    groups, tap_count = key_taps.shape
    group_size = channels // groups
    ctx_index = lax.axis_index("ctx")
    width_all = channels * lax.axis_size("ch")
    rim = tap_count - 1
    tails = passed_along((key_proj[tok_rows - rim :], value_proj[tok_rows - rim :]), "ctx", 1)
    key_spread = jnp.repeat(key_taps.astype(jnp.float32), group_size, axis=0)
    value_spread = jnp.repeat(value_taps.astype(jnp.float32), group_size, axis=0)
    key_mixed, key_extended = short_apply(key_proj, tails[0], key_spread)
    value_mixed, value_extended = short_apply(value_proj, tails[1], value_spread)
    product = (key_mixed * value_mixed).astype(jnp.bfloat16)
    product_wide = product.astype(jnp.float32)
    product_blocks = product_wide.reshape(tok_rows, groups, group_size)
    rates = decay_rates[:, :, None]
    positions = jnp.arange(tok_rows).astype(jnp.float32)
    lag_index = jnp.arange(tok_rows)[:, None] - jnp.arange(tok_rows)[None, :]
    filt_rows = jnp.sum(residues[:, :, None] * jnp.exp(-rates * positions[None, None, :]), axis=1)
    triangle = jnp.where(
        lag_index[None] >= 0, filt_rows[:, jnp.clip(lag_index, 0, tok_rows - 1)], 0.0
    )
    enter_weights = residues[:, :, None] * jnp.exp(-rates * (positions + 1.0)[None, None, :])
    leave_weights = residues[:, :, None] * jnp.exp(-rates * (tok_rows - positions)[None, None, :])
    local_forward = jnp.einsum("gts,sgc->tgc", triangle, product_blocks, precision=HIGHEST)
    end_weights = jnp.exp(-rates * (tok_rows - 1.0 - positions)[None, None, :])
    own_end = jnp.einsum("gms,sgc->gmc", end_weights, product_blocks, precision=HIGHEST)
    piece = lax.all_gather(own_end[None], "ctx", axis=0, tiled=True)
    count = piece.shape[0]
    steps = ctx_index - 1 - jnp.arange(count)
    spans = (jnp.maximum(steps, 0) * tok_rows).astype(jnp.float32)
    weights = jnp.where(steps[None, None, :] >= 0, jnp.exp(-rates * spans[None, None, :]), 0.0)
    incoming = jnp.einsum("gmk,kgmc->gmc", weights, piece, precision=HIGHEST)
    remote_forward = jnp.einsum("gmt,gmc->tgc", enter_weights, incoming, precision=HIGHEST)
    long_part = (local_forward + remote_forward).reshape(tok_rows, channels)
    mixed = long_part + skip_weight * product_wide
    query_wide = query_proj.astype(jnp.float32)
    gated = query_wide * mixed
    grad_wide = out_grad.astype(jnp.float32)
    squares, projected = lax.psum(
        (jnp.sum(gated * gated, axis=1), jnp.sum(gated * norm_gain * grad_wide, axis=1)), "ch"
    )
    scaled = lax.rsqrt(squares / width_all + EPSILON)[:, None]
    mixed_out = (gated * scaled * norm_gain).astype(jnp.bfloat16)
    gated_grad = scaled * norm_gain * grad_wide - gated * (
        scaled * scaled * scaled * projected[:, None] / width_all
    )
    gain_part = jnp.sum(grad_wide * gated * scaled, axis=0)
    query_grad = (gated_grad * mixed).astype(jnp.bfloat16)
    mixed_grad = (gated_grad * query_wide).astype(jnp.bfloat16)
    mixed_grad_wide = mixed_grad.astype(jnp.float32)
    grad_blocks = mixed_grad_wide.reshape(tok_rows, groups, group_size)
    local_backward = jnp.einsum("gts,tgc->sgc", triangle, grad_blocks, precision=HIGHEST)
    begin_weights = jnp.exp(-rates * positions[None, None, :])
    own_begin = jnp.einsum("gmt,tgc->gmc", begin_weights, grad_blocks, precision=HIGHEST)
    piece = lax.all_gather(own_begin[None], "ctx", axis=0, tiled=True)
    count = piece.shape[0]
    steps = jnp.arange(count) - ctx_index - 1
    spans = (jnp.maximum(steps, 0) * tok_rows).astype(jnp.float32)
    weights = jnp.where(steps[None, None, :] >= 0, jnp.exp(-rates * spans[None, None, :]), 0.0)
    incoming_back = jnp.einsum("gmk,kgmc->gmc", weights, piece, precision=HIGHEST)
    remote_backward = jnp.einsum("gms,gmc->sgc", leave_weights, incoming_back, precision=HIGHEST)
    long_back = (local_backward + remote_backward).reshape(tok_rows, channels)
    product_grad = long_back + skip_weight * mixed_grad_wide
    skip_part = jnp.sum(mixed_grad_wide * product_wide, axis=0)
    key_mixed_grad = (product_grad * value_mixed).astype(jnp.bfloat16)
    value_mixed_grad = (product_grad * key_mixed).astype(jnp.bfloat16)
    heads = passed_along((key_mixed_grad[:rim], value_mixed_grad[:rim]), "ctx", -1)
    key_grad = short_adjoint(key_mixed_grad, heads[0], key_spread).astype(jnp.bfloat16)
    value_grad = short_adjoint(value_mixed_grad, heads[1], value_spread).astype(jnp.bfloat16)
    key_taps_part = taps_gradient(key_mixed_grad, key_extended, groups, tap_count)
    value_taps_part = taps_gradient(value_mixed_grad, value_extended, groups, tap_count)
    summed = lax.psum((key_taps_part, value_taps_part, skip_part, gain_part), "ctx")
    return (mixed_out, query_grad, key_grad, value_grad, summed[0], summed[1], summed[2], summed[3])


def solution(mesh):
    placed = (
        P("ctx", "ch"),
        P("ctx", "ch"),
        P("ctx", "ch"),
        P("ch", None),
        P("ch", None),
        P("ch", None),
        P("ch", None),
        P("ch"),
        P("ch"),
        P("ctx", "ch"),
    )
    return jax.shard_map(
        local,
        mesh=mesh,
        in_specs=placed,
        out_specs=(
            P("ctx", "ch"),
            P("ctx", "ch"),
            P("ctx", "ch"),
            P("ctx", "ch"),
            P("ch", None),
            P("ch", None),
            P("ch"),
            P("ch"),
        ),
        check_vma=False,
    )
```

profile of v0, /device:TPU:0, one launch (start us, length us, event | category | flops | bytes accessed | tf_op | source)
XLA Modules:
  0.0 345.9 jit_solution(14882163737550079523)
XLA Ops:
  7.2 0.9 slice.85
  8.2 2.4 collective-permute-start.1
  10.5 0.9 slice.78
  11.4 4.5 %collective-permute-start = (bf16[2,4096]{1,0:T(2,128)(2,1)S(1)}, bf16[2,4096]{1,0:T(2,128)(2,1)S(1)}, u32[]{:S(2)}, u32[]{:S(2)}) collective-permute-start(bf16[2,4096]{1,0:T(2,128)(2,1)S(1)} %slice.78), channel_id=1, source_target_pairs={{0,2},{2,4},{4,6},{6,8},{8,10},{10,12},{12,14},{14,16},{16,18},{18... | collective-permute-start | bytes 49160 | tf_op jit(solution)/shard_map/ppermute | solution.py:13
  15.9 0.8 broadcast_in_dim.39
  17.1 0.8 broadcast_in_dim.38
  18.9 1.6 copy.81
  21.2 2.7 maximum_convert_fusion.1
  24.4 0.8 maximum_convert_fusion
  25.2 2.5 copy-done
  27.7 7.1 %multiply_convert_fusion.4 = (bf16[128,4096]{0,1:T(8,128)(2,1)S(1)}, f32[128,4096]{0,1:T(8,128)}, f32[128,4096]{0,1:T(8,128)}) fusion(f32[4096]{0:T(1024)S(1)} %bitcast.84, f32[130,4096]{0,1:T(8,128)S(1)} %copy-done, f32[4096]{0:T(1024)S(1)} %bitcast.86, f32[4096]{0:T(1024)S(1)} %bitcast.82, f32[4096]{0:T(1024)S(1)} %bitcast.90, ...), kind=kLoop, calls=%fused_computation.76 | loop fusion | flops 6291456 | bytes 17924096 | tf_op jit(solution)/shard_map/convert_element_type | solution.py:71
  34.9 1.9 fusion.38
  36.7 1.7 copy.88
  38.7 2.3 copy.79
  41.6 1.7 multiply_reduce_fusion.3
  43.4 61.7 %gather_fusion = f32[16384,256]{1,0:T(8,128)} fusion(f32[256,128]{0,1:T(8,128)S(1)} %copy.86, s32[16384]{0:T(1024)S(1)} %fusion.59), kind=kCustom, calls=%fused_computation | custom fusion | bytes 33619968 | tf_op jit(solution)/shard_map/gather | solution.py:79
  105.1 18.1 %copy.87 = f32[128,128,256]{1,0,2:T(8,128)} copy(f32[128,128,256]{2,1,0:T(8,128)} %bitcast.71) | data formatting | bytes 33554432 | tf_op jit(solution)/shard_map/gather | solution.py:79
  123.2 1.3 copy.89
  124.6 0.8 exponential_select_fusion
  125.4 16.5 %fusion.2 = f32[256,16,128]{2,1,0:T(8,128)} fusion(bf16[128,256,16]{0,2,1:T(8,128)(2,1)S(1)} %bitcast.73, f32[128,128,256]{1,0,2:T(8,128)} %copy.87, pred[128,128]{1,0:T(8,128)(4,1)S(1)} %subtract_compare_fusion), kind=kOutput, calls=%fused_computation.3 | convolution fusion | flops 809500672 | bytes 19939328 | tf_op jit(solution)/shard_map/gts,sgc->tgc/dot_general | solution.py:83
  141.9 3.9 %copy.115 = f32[32,8,16,256]{3,2,1,0:T(8,128)S(1)} copy(f32[32,8,16,256]{3,1,2,0:T(8,128)} %bitcast.80) | data formatting | bytes 8388608
  145.8 1.1 multiply_reduce_fusion.1
  146.9 2.5 copy.105
  149.4 4.5 %fusion.42 = f32[256,16,128]{2,1,0:T(8,128)S(1)} fusion(f32[256,16,128]{2,1,0:T(8,128)} %fusion.2, f32[256,16,16]{1,2,0:T(8,128)} %copy.105, f32[128]{0:T(128)S(1)} %broadcast_add_fusion, f32[256,16]{1,0:T(8,128)S(1)} %copy.85, f32[256,16]{1,0:T(8,128)S(1)} %copy.84), kind=kOutput, calls=%fused_computation.79 | convolution fusion | flops 102236160 | bytes 4489728 | tf_op jit(solution)/shard_map/gmt,gmc->tgc/dot_general | solution.py:92
  154.0 2.4 multiply_reduce_fusion.2
  156.4 5.5 %psum.42 = f32[128]{0:T(128)} all-reduce(f32[128]{0:T(128)} %get-tuple-element.56), channel_id=1, replica_groups=mesh['ctx'=16,'ch'=2] {'ch'}, use_global_device_ids=true, to_apply=%region_2.3 | all-reduce | flops 128 | bytes 1024 | tf_op jit(solution)/shard_map/psum | solution.py:98
  163.1 3.2 fusion.17
  166.4 5.8 %psum.43 = f32[128]{0:T(128)} all-reduce(f32[128]{0:T(128)} %get-tuple-element.47), channel_id=1, replica_groups=mesh['ctx'=16,'ch'=2] {'ch'}, use_global_device_ids=true, to_apply=%region_4.5 | all-reduce | flops 128 | bytes 1024 | tf_op jit(solution)/shard_map/psum | solution.py:98
  172.8 5.0 %fusion.13 = (f32[4096]{0:T(1024)}, bf16[128,4096]{0,1:T(8,128)(2,1)S(1)}, bf16[128,4096]{0,1:T(8,128)(2,1)}, bf16[128,4096]{0,1:T(8,128)(2,1)}) fusion(bf16[128,4096]{0,1:T(8,128)(2,1)S(1)} %get-tuple-element.58, bf16[128,4096]{0,1:T(8,128)(2,1)} %copy.79, f32[128,4096]{0,1:T(8,128)} %get-tuple-element.57, f32[128]{0:T(128)S(1)} %fusion.62, ...), kind=kLoop, calls=%fused_computation.30 | loop fusion | flops 9957376 | bytes 10535936 | tf_op jit(solution)/shard_map/reduce_sum | solution.py:123
  177.8 1.0 copy-done.3
  178.8 1.9 fusion.41
  180.7 1.7 copy.90
  182.5 2.4 copy.95
  184.8 1.3 copy.96
  186.1 11.9 %fusion = f32[256,16,128]{2,1,0:T(8,128)} fusion(bf16[128,256,16]{0,2,1:T(8,128)(2,1)S(1)} %bitcast.77, f32[128,128,256]{1,0,2:T(8,128)} %copy.87, pred[128,128]{1,0:T(8,128)(4,1)S(1)} %subtract_compare_fusion), kind=kOutput, calls=%fused_computation.1 | convolution fusion | flops 809500672 | bytes 19939328 | tf_op jit(solution)/shard_map/gts,tgc->sgc/dot_general | solution.py:111
  198.1 38.1 %all-gather.7.cloned.1.call-done = f32[4096,16,16]{0,2,1:T(8,128)} async-done(((f32[256,16,16]{0,2,1:T(8,128)}), f32[4096,16,16]{0,2,1:T(8,128)}) %all-gather.7.cloned.1.call-update) | async-done | bytes 4194320 | tf_op jit(solution)/shard_map/all_gather | solution.py:114
  236.1 4.0 %copy.116 = f32[32,8,16,256]{3,2,1,0:T(8,128)S(1)} copy(f32[32,8,16,256]{3,1,2,0:T(8,128)} %bitcast.81) | data formatting | bytes 8388608
  240.1 1.8 multiply_reduce_fusion
  241.9 2.3 copy.112
  244.2 4.8 %fusion.45 = f32[256,16,128]{2,1,0:T(8,128)S(1)} fusion(f32[256,16,128]{2,1,0:T(8,128)} %fusion, f32[256,16,16]{1,2,0:T(8,128)S(1)} %copy.112, f32[128]{0:T(128)S(1)} %broadcast_subtract_fusion, f32[256,16]{1,0:T(8,128)S(1)} %copy.85, f32[256,16]{1,0:T(8,128)S(1)} %copy.84), kind=kOutput, calls=%fused_computation.80 | convolution fusion | flops 102236160 | bytes 4489728 | tf_op jit(solution)/shard_map/gms,gmc->sgc/dot_general | solution.py:120
  249.1 11.8 %fusion.21 = (f32[4096]{0:T(1024)S(1)}, f32[4096]{0:T(1024)S(1)}, f32[4096]{0:T(1024)S(1)}, bf16[128,4096]{0,1:T(8,128)(2,1)S(1)}, f32[4096]{0:T(1024)S(1)}, /*i...) fusion(f32[130,4096]{0,1:T(8,128)S(1)} %copy-done.1, f32[128,4096]{0,1:T(8,128)} %get-tuple-element.60, ...), kind=kLoop, calls=%fused_computation.38 | loop fusion | flops 10985472 | bytes 22134784 | tf_op jit(solution)/shard_map/reduce_sum | solution.py:43
  261.3 1.3 collective-permute-start.2
  263.0 1.3 collective-permute-start.3
  265.6 62.2 %all-reduce = (f32[256,3]{0,1:T(4,128)}, f32[256,3]{0,1:T(4,128)}, f32[4096]{0:T(1024)}, f32[4096]{0:T(1024)}) all-reduce(f32[256,3]{0,1:T(4,128)S(1)} %pad_maximum_fusion, f32[256,3]{0,1:T(4,128)S(1)} %pad_maximum_fusion.1, f32[4096]{0:T(1024)S(1)} %copy-done.14, f32[4096]{0:T(1024)S(1)} %copy-done.13), channel_id=1, replica_groups=mesh['ctx'=16,'ch'=2] {'ctx'}, use_global_device_ids=true, to_apply=%region_11.12 | all-reduce | flops 9728 | bytes 77824 | tf_op jit(solution)/shard_map/psum | solution.py:131
  328.7 3.2 fusion.28
  331.9 1.3 copy.97
  334.1 3.2 fusion.25
  337.3 1.3 copy.98
  (88 shorter events, 9.1 us)
Async XLA Ops:
  7.2 11.1 %copy-start.8 = (bf16[128,4096]{1,0:T(8,128)(2,1)S(1)}, bf16[128,4096]{1,0:T(8,128)(2,1)}, u32[]{:S(2)}) copy-start(bf16[128,4096]{1,0:T(8,128)(2,1)} %param.12) | copy-start | bytes 3145732
  7.2 134.7 %all-gather.5.cloned.1.call-start = ((), (), s32[]{:S(2)}) async-start(), calls=%async_computation | async-start | bytes 4456448 | tf_op jit(solution)/shard_map/all_gather | solution.py:86
  8.2 12.5 %collective-permute-start.1 = (bf16[2,4096]{1,0:T(2,128)(2,1)S(1)}, bf16[2,4096]{1,0:T(2,128)(2,1)S(1)}, u32[]{:S(2)}, u32[]{:S(2)}) collective-permute-start(bf16[2,4096]{1,0:T(2,128)(2,1)S(1)} %slice.85), channel_id=1, source_target_pairs={{0,2},{2,4},{4,6},{6,8},{8,10},{10,12},{12,14},{14,16},{16,18},{18... | collective-permute-start | bytes 49160 | tf_op jit(solution)/shard_map/ppermute | solution.py:13
  11.4 12.5 %collective-permute-start = (bf16[2,4096]{1,0:T(2,128)(2,1)S(1)}, bf16[2,4096]{1,0:T(2,128)(2,1)S(1)}, u32[]{:S(2)}, u32[]{:S(2)}) collective-permute-start(bf16[2,4096]{1,0:T(2,128)(2,1)S(1)} %slice.78), channel_id=1, source_target_pairs={{0,2},{2,4},{4,6},{6,8},{8,10},{10,12},{12,14},{14,16},{16,18},{18... | collective-permute-start | bytes 49160 | tf_op jit(solution)/shard_map/ppermute | solution.py:13
  18.2 2.3 copy-start.16
  24.4 3.3 copy-start
  25.2 9.6 %copy-start.2 = (f32[130,4096]{0,1:T(8,128)}, f32[130,4096]{0,1:T(8,128)S(1)}, u32[]{:S(2)}) copy-start(f32[130,4096]{0,1:T(8,128)S(1)} %maximum_convert_fusion) | copy-start | bytes 6389764
  36.7 4.2 %copy-start.15 = (f32[256,16]{0,1:T(8,128)S(1)}, f32[256,16]{0,1:T(8,128)}, u32[]{:S(2)}) copy-start(f32[256,16]{0,1:T(8,128)} %param.15) | copy-start | bytes 49156
  38.5 197.7 %all-gather.7.cloned.1.call-start = ((), (), s32[]{:S(2)}) async-start(), calls=%async_computation.1 | async-start | bytes 4456448 | tf_op jit(solution)/shard_map/all_gather | solution.py:114
  41.1 0.5 copy-start.18
  105.1 18.1 %copy-start.10 = (bf16[128,4096]{1,0:T(8,128)(2,1)S(1)}, bf16[128,4096]{1,0:T(8,128)(2,1)}, u32[]{:S(2)}) copy-start(bf16[128,4096]{1,0:T(8,128)(2,1)} %param.19) | copy-start | bytes 3145732
  149.4 4.5 %copy-start.5 = (bf16[128,4096]{0,1:T(8,128)(2,1)S(1)}, bf16[128,4096]{0,1:T(8,128)(2,1)}, u32[]{:S(2)}) copy-start(bf16[128,4096]{0,1:T(8,128)(2,1)} %copy.79) | copy-start | bytes 3145732
  149.4 4.5 %copy-start.11 = (f32[4096]{0:T(1024)S(1)}, f32[4096]{0:T(1024)}, u32[]{:S(2)}) copy-start(f32[4096]{0:T(1024)} %param.17) | copy-start | bytes 49156
  153.9 9.2 %copy-start.12 = (f32[4096]{0:T(1024)S(1)}, f32[4096]{0:T(1024)}, u32[]{:S(2)}) copy-start(f32[4096]{0:T(1024)} %param.18) | copy-start | bytes 49156
  162.6 0.5 copy-start.17
  172.8 6.0 %copy-start.19 = (f32[128]{0:T(128)S(1)}, f32[128]{0:T(128)}, u32[]{:S(2)}) copy-start(f32[128]{0:T(128)} %copy-done.18) | copy-start | bytes 1540
  177.8 1.0 copy-start.3
  180.7 4.1 %copy-start.7 = (bf16[128,4096]{0,1:T(8,128)(2,1)S(1)}, bf16[128,4096]{0,1:T(8,128)(2,1)}, u32[]{:S(2)}) copy-start(bf16[128,4096]{0,1:T(8,128)(2,1)} %get-tuple-element.61) | copy-start | bytes 3145732
  182.5 3.7 %copy-start.4 = (bf16[128,4096]{0,1:T(8,128)(2,1)S(1)}, bf16[128,4096]{0,1:T(8,128)(2,1)}, u32[]{:S(2)}) copy-start(bf16[128,4096]{0,1:T(8,128)(2,1)} %copy-done.3) | copy-start | bytes 3145732
  236.1 4.0 %copy-start.9 = (f32[256,16,16]{0,2,1:T(8,128)S(1)}, f32[256,16,16]{0,2,1:T(8,128)}, u32[]{:S(2)}) copy-start(f32[256,16,16]{0,2,1:T(8,128)} %get-tuple-element.73) | copy-start | bytes 786436
  244.2 4.9 %copy-start.1 = (f32[130,4096]{0,1:T(8,128)S(1)}, f32[130,4096]{0,1:T(8,128)}, u32[]{:S(2)}) copy-start(f32[130,4096]{0,1:T(8,128)} %maximum_convert_fusion.1) | copy-start | bytes 6389764
  244.2 4.9 %copy-start.6 = (f32[128,4096]{0,1:T(8,128)S(1)}, f32[128,4096]{0,1:T(8,128)}, u32[]{:S(2)}) copy-start(f32[128,4096]{0,1:T(8,128)} %get-tuple-element.59) | copy-start | bytes 6291460
  260.9 4.7 %copy-start.13 = (f32[4096]{0:T(1024)S(1)}, f32[4096]{0:T(1024)}, u32[]{:S(2)}) copy-start(f32[4096]{0:T(1024)} %get-tuple-element.46) | copy-start | bytes 49156
  260.9 4.7 %copy-start.14 = (f32[4096]{0:T(1024)S(1)}, f32[4096]{0:T(1024)}, u32[]{:S(2)}) copy-start(f32[4096]{0:T(1024)} %get-tuple-element.52) | copy-start | bytes 49156
  261.3 66.6 %collective-permute-start.2 = (bf16[2,4096]{1,0:T(2,128)(2,1)S(1)}, bf16[2,4096]{1,0:T(2,128)(2,1)S(1)}, u32[]{:S(2)}, u32[]{:S(2)}) collective-permute-start(bf16[2,4096]{1,0:T(2,128)(2,1)S(1)} %copy.91), channel_id=1, source_target_pairs={{2,0},{4,2},{6,4},{8,6},{10,8},{12,10},{14,12},{16,14},{18,16},{20... | collective-permute-start | bytes 49160 | tf_op jit(solution)/shard_map/ppermute | solution.py:13
  263.0 70.2 %collective-permute-start.3 = (bf16[2,4096]{1,0:T(2,128)(2,1)S(1)}, bf16[2,4096]{1,0:T(2,128)(2,1)S(1)}, u32[]{:S(2)}, u32[]{:S(2)}) collective-permute-start(bf16[2,4096]{1,0:T(2,128)(2,1)S(1)} %copy.93), channel_id=1, source_target_pairs={{2,0},{4,2},{6,4},{8,6},{10,8},{12,10},{14,12},{16,14},{18,16},{20... | collective-permute-start | bytes 49160 | tf_op jit(solution)/shard_map/ppermute | solution.py:13
Sparse Core Ops, SparseCore 0:
  38.6 53.5 all-gather.4
  182.6 53.5 all-gather.6
where the time goes:
time: 352 us; the launch traced here: 346 us
  local copies, waits for them, and re-layouts  120 us (34%)
  blocking collectives  73.5 us (21%)
  other arithmetic  47.6 us (14%)
  matrix products  41.5 us (12%)
  waiting for transfers between devices  38.1 us (11%)
  between operations  15 us (4%)
  starting transfers between devices  9.73 us (3%)
    gather x2, local copies, waits for them, and re-layouts, local(): filt_rows[:, jnp.clip(lag_index, 0, tok_rows - 1)]  79.8 us
    psum x1, blocking collectives, local(): lax.psum((key_taps_part, value_taps_part, skip_part, gain_part), 'ctx')  62.2 us
    all_gather x1, waiting for transfers between devices, local(): piece = lax.all_gather(own_begin[None], 'ctx', axis=0, tiled=True)  38.1 us
    unnamed x51, local copies, waits for them, and re-layouts  24.7 us
    dot_general x1, matrix products, local(): jnp.einsum('gts,sgc->tgc', triangle, product_blocks, precision=HIGHEST)  16.5 us
    dot_general x1, matrix products, local(): jnp.einsum('gts,tgc->sgc', triangle, grad_blocks, precision=HIGHEST)  11.9 us
    reduce_sum x1, other arithmetic, taps_gradient(): per_channel = jnp.sum(grad_wide * extended[begin:begin + tok_rows], axis=0)  11.8 us
    psum x2, blocking collectives, local(): lax.psum((jnp.sum(gated * gated, axis=1), jnp.sum(gated * norm_gain * gra...  11.3 us
  transfers between devices with their start and end apart: 6, of which 1 were waited for; matrix products, arithmetic and copies ran while one was open for 39% of the time, Pallas kernels for 0%

commit v1 on v0

v1 whole, which is shorter than its diff:
```python
import functools

import jax
import jax.numpy as jnp
from jax import lax
from jax.experimental import pallas as pl
from jax.experimental.pallas import tpu as pltpu
from jax.sharding import PartitionSpec as P

EPSILON = 1e-06
TILE = 256
F32, BF16 = jnp.float32, jnp.bfloat16


def halves(wide):
    high = wide.astype(BF16)
    return high, (wide - high.astype(F32)).astype(BF16)


def contract_rows(weights, signal):
    return lax.dot_general(weights, signal, (((0,), (0,)), ((), ())), preferred_element_type=F32)


def body(
    n, n_ch, slices, width_all, group_size,
    q_ref, k_ref, v_ref, og_ref, prm_ref, rate_ref, filt_ref, turned_ref,
    out_ref, qg_ref, kg_ref, vg_ref, sum_ref,
    tail_out, tail_in, head_out, head_in,
    prod, kmix, vmix, mixed, mgrad, kmg, vmg,
    own, gathered, prefix, incoming,
    own_b, gathered_b, suffix, incoming_b,
    part, parts, total,
    row_acc, row_out, row_in,
    tail_sem, head_sem, send_sem, recv_sem, ch_send, ch_recv,
):
    me = lax.axis_index("ctx")
    me_ch = lax.axis_index("ch")
    rows = q_ref.shape[0]

    def to_ctx(src, dst, s_sem, r_sem, peer):
        return pltpu.make_async_remote_copy(
            src_ref=src, dst_ref=dst, send_sem=s_sem, recv_sem=r_sem,
            device_id={"ctx": peer}, device_id_type=pl.DeviceIdType.MESH,
        )

    def columns(j):
        return pl.ds(pl.multiple_of(j * TILE, TILE), TILE)

    barrier = pltpu.get_barrier_semaphore()

    @pl.loop(1, n)
    def _(i):
        pl.semaphore_signal(
            barrier, inc=1, device_id={"ctx": lax.rem(me + i, n)},
            device_id_type=pl.DeviceIdType.MESH,
        )

    for i in range(1, n_ch):
        pl.semaphore_signal(
            barrier, inc=1, device_id={"ch": lax.rem(me_ch + i, n_ch)},
            device_id_type=pl.DeviceIdType.MESH,
        )
    tail_out[0:2] = k_ref[rows - 16 : rows].astype(F32)[14:16]
    tail_out[2:4] = v_ref[rows - 16 : rows].astype(F32)[14:16]
    pl.semaphore_wait(barrier, n - 1 + n_ch - 1)

    tails = to_ctx(tail_out, tail_in, tail_sem.at[0], tail_sem.at[1], lax.rem(me + 1, n))
    heads = to_ctx(head_out, head_in, head_sem.at[0], head_sem.at[1], lax.rem(me + n - 1, n))

    @pl.when(me < n - 1)
    def _():
        tails.start()

    @pl.when(me == 0)
    def _():
        tail_in[...] = jnp.zeros(tail_in.shape, F32)

    @pl.when(me > 0)
    def _():
        tails.wait_recv()

    row = lax.broadcasted_iota(jnp.int32, (rows, TILE), 0)
    row_wide = row.astype(F32)
    lane_group = lax.broadcasted_iota(jnp.int32, (rows, TILE), 1) // group_size
    block_mask = (
        lax.broadcasted_iota(jnp.int32, (TILE, TILE), 0) // group_size
        == lax.broadcasted_iota(jnp.int32, (TILE, TILE), 1) // group_size
    )
    tri_row = lax.broadcasted_iota(jnp.int32, (rows, rows), 0)
    tri_col = lax.broadcasted_iota(jnp.int32, (rows, rows), 1)
    groups_tile = TILE // group_size

    def delayed(ref, cols, base):
        wide = ref[:, cols].astype(F32)
        older = tail_in[base : base + 1, cols]
        newer = tail_in[base + 1 : base + 2, cols]
        one = jnp.where(row == 0, newer, pltpu.roll(wide, 1, 0))
        two = jnp.where(row == 0, older, jnp.where(row == 1, newer, pltpu.roll(wide, 2, 0)))
        return wide, one, two

    def modal(weights, signal):
        high, low = halves(weights)
        full = contract_rows(
            jnp.concatenate([high, low], axis=0), jnp.concatenate([signal, signal], axis=0)
        )
        kept = jnp.where(block_mask, full, 0.0)
        return jnp.sum(kept.reshape(groups_tile, group_size, TILE), axis=0)

    def spread(weights, state):
        high, low = halves(weights)
        tiled = jnp.where(block_mask, jnp.concatenate([state] * groups_tile, axis=0), 0.0)
        s_high, s_low = halves(tiled)
        return jnp.dot(
            jnp.concatenate([high, low, high], axis=1),
            jnp.concatenate([s_high, s_high, s_low], axis=0),
            preferred_element_type=F32,
        )

    def toeplitz(table, j, signal, keep):
        lines = table[pl.ds(pl.multiple_of(j * groups_tile, groups_tile), groups_tile), :]
        wide = signal.astype(F32)
        lhs, rhs = [], []
        for g in range(groups_tile):
            spread_line = jnp.broadcast_to(lines[g : g + 1, :], (rows, rows))
            turned = pltpu.roll(spread_line, 0, 1, stride=1, stride_axis=0)
            lhs.append(jnp.where(keep, turned, 0.0).astype(BF16))
            rhs.append(jnp.where(lane_group == g, wide, 0.0).astype(BF16))
        return jnp.dot(
            jnp.concatenate(lhs, axis=1), jnp.concatenate(rhs, axis=0),
            preferred_element_type=F32,
        )

    def scatter(phase, source, target, j):
        copy = to_ctx(
            source.at[j], target.at[me], send_sem.at[phase, j], recv_sem.at[phase, me], j
        )

        @pl.when(j != me)
        def _():
            copy.start()

        @pl.when(j == me)
        def _():
            target[me] = source[j]

    def arrive(phase, source, target, i):
        @pl.when(i != me)
        def _():
            to_ctx(
                source.at[0], target.at[i], send_sem.at[phase, 0], recv_sem.at[phase, i], i
            ).wait_recv()

    def sent(phase, source, target, count):
        @pl.loop(0, count)
        def _(j):
            @pl.when(j != me)
            def _():
                to_ctx(
                    source.at[j], target.at[me], send_sem.at[phase, j], recv_sem.at[phase, me], j
                ).wait_send()

    @pl.loop(0, slices)
    def _(i):
        j = lax.rem(me + i, slices)
        cols = columns(j)
        k0, k1, k2 = delayed(k_ref, cols, 0)
        key = k0 * prm_ref[0:1, cols] + k1 * prm_ref[1:2, cols] + k2 * prm_ref[2:3, cols]
        v0, v1, v2 = delayed(v_ref, cols, 2)
        value = v0 * prm_ref[3:4, cols] + v1 * prm_ref[4:5, cols] + v2 * prm_ref[5:6, cols]
        kmix[:, cols] = key
        vmix[:, cols] = value
        product = (key * value).astype(BF16)
        prod[:, cols] = product
        own[j] = modal(jnp.exp(-prm_ref[8:9, cols] * (rows - 1.0 - row_wide)), product)
        scatter(0, own, gathered, j)

    def long_forward(j):
        cols = columns(j)
        product = prod[:, cols]
        mixed[:, cols] = (
            toeplitz(turned_ref, j, product, tri_row >= tri_col)
            + prm_ref[6:7, cols] * product.astype(F32)
        )

    early = slices // 2

    @pl.loop(0, early)
    def _(j):
        long_forward(j)

    @pl.when(me < slices)
    def _():
        fall = jnp.exp(-rate_ref[:, columns(me)] * float(rows))

        def step(i, carry):
            prefix[i] = carry
            scatter(1, prefix, incoming, i)
            arrive(0, own, gathered, i)
            return fall * carry + gathered[i]

        lax.fori_loop(0, n, step, jnp.zeros((group_size, TILE), F32))

    @pl.loop(early, slices)
    def _(j):
        long_forward(j)

    row_acc[...] = jnp.zeros(row_acc.shape, F32)

    @pl.loop(0, slices)
    def _(i):
        j = lax.rem(me + i, slices)
        cols = columns(j)
        arrive(1, prefix, incoming, j)
        enter = prm_ref[9:10, cols] * jnp.exp(-prm_ref[8:9, cols] * (row_wide + 1.0))
        full = mixed[:, cols] + spread(enter, incoming[j])
        mixed[:, cols] = full
        gated = q_ref[:, cols].astype(F32) * full
        squares = gated * gated
        along = gated * prm_ref[7:8, cols] * og_ref[:, cols].astype(F32)
        row_acc[0] += squares[:, :128] + squares[:, 128:]
        row_acc[1] += along[:, :128] + along[:, 128:]

    lane = lax.broadcasted_iota(jnp.int32, (rows, 128), 1)
    squares = jnp.sum(row_acc[0], axis=1, keepdims=True)
    along = jnp.sum(row_acc[1], axis=1, keepdims=True)
    row_out[...] = jnp.where(lane == 0, squares, along)

    def to_ch(i):
        return pltpu.make_async_remote_copy(
            src_ref=row_out, dst_ref=row_in.at[i - 1], send_sem=ch_send.at[i - 1],
            recv_sem=ch_recv.at[i - 1], device_id={"ch": lax.rem(me_ch + i, n_ch)},
            device_id_type=pl.DeviceIdType.MESH,
        )

    for i in range(1, n_ch):
        to_ch(i).start()
    summed = row_out[...]
    for i in range(1, n_ch):
        to_ch(i).wait_recv()
        summed = summed + row_in[i - 1]
    squares, along = summed[:, 0:1], summed[:, 1:2]
    scaled = lax.rsqrt(squares / width_all + EPSILON)
    pull = scaled * scaled * scaled * along / width_all

    @pl.loop(0, slices)
    def _(i):
        j = lax.rem(me + i, slices)
        cols = columns(j)
        gain = prm_ref[7:8, cols]
        query = q_ref[:, cols].astype(F32)
        grad = og_ref[:, cols].astype(F32)
        full = mixed[:, cols]
        normed = query * full * scaled
        out_ref[:, cols] = (normed * gain).astype(BF16)
        gated_grad = scaled * gain * grad - query * full * pull
        qg_ref[:, cols] = (gated_grad * full).astype(BF16)
        mixed_grad = (gated_grad * query).astype(BF16)
        mgrad[:, cols] = mixed_grad
        mixed_wide = mixed_grad.astype(F32)
        part[j, 0:1, :] = jnp.sum(mixed_wide * prod[:, cols].astype(F32), axis=0, keepdims=True)
        part[j, 1:2, :] = jnp.sum(grad * normed, axis=0, keepdims=True)
        own_b[j] = modal(jnp.exp(-prm_ref[8:9, cols] * row_wide), mixed_grad)
        scatter(2, own_b, gathered_b, j)

    def long_backward(j):
        cols = columns(j)
        grad = mgrad[:, cols]
        mixed[:, cols] = (
            toeplitz(filt_ref, j, grad, tri_row <= tri_col)
            + prm_ref[6:7, cols] * grad.astype(F32)
        )

    @pl.loop(0, early)
    def _(j):
        long_backward(j)

    @pl.when(me < slices)
    def _():
        fall = jnp.exp(-rate_ref[:, columns(me)] * float(rows))

        def step(i, carry):
            place = n - 1 - i
            suffix[place] = carry
            scatter(3, suffix, incoming_b, place)
            arrive(2, own_b, gathered_b, place)
            return fall * carry + gathered_b[place]

        lax.fori_loop(0, n, step, jnp.zeros((group_size, TILE), F32))

    @pl.loop(early, slices)
    def _(j):
        long_backward(j)

    @pl.loop(0, slices)
    def _(i):
        j = lax.rem(me + i, slices)
        cols = columns(j)
        arrive(3, suffix, incoming_b, j)
        leave = prm_ref[9:10, cols] * jnp.exp(-prm_ref[8:9, cols] * (rows - row_wide))
        pgrad = mixed[:, cols] + spread(leave, incoming_b[j])
        key_grad = (pgrad * vmix[:, cols]).astype(BF16)
        value_grad = (pgrad * kmix[:, cols]).astype(BF16)
        kmg[:, cols] = key_grad
        vmg[:, cols] = value_grad
        key_wide, value_wide = key_grad.astype(F32), value_grad.astype(F32)
        head_out[0:2, cols] = key_wide[0:2]
        head_out[2:4, cols] = value_wide[0:2]
        for offset, window in enumerate(delayed(k_ref, cols, 0)):
            part[j, 2 + offset : 3 + offset, :] = jnp.sum(key_wide * window, axis=0, keepdims=True)
        for offset, window in enumerate(delayed(v_ref, cols, 2)):
            part[j, 5 + offset : 6 + offset, :] = jnp.sum(value_wide * window, axis=0, keepdims=True)
        scatter(4, part, parts, j)

    @pl.when(me > 0)
    def _():
        heads.start()

    @pl.when(me == n - 1)
    def _():
        head_in[...] = jnp.zeros(head_in.shape, F32)

    @pl.when(me < slices)
    def _():
        def step(i, carry):
            arrive(4, part, parts, i)
            return carry + parts[i]

        total[me] = lax.fori_loop(0, n, step, jnp.zeros((8, TILE), F32))

        @pl.loop(0, n)
        def _(i):
            @pl.when(i != me)
            def _():
                to_ctx(
                    total.at[me], total.at[me], send_sem.at[5, i], recv_sem.at[5, me], i
                ).start()

    @pl.when(me < n - 1)
    def _():
        heads.wait_recv()

    def advanced(ref, cols, base):
        wide = ref[:, cols].astype(F32)
        first = head_in[base : base + 1, cols]
        second = head_in[base + 1 : base + 2, cols]
        one = jnp.where(row == rows - 1, first, pltpu.roll(wide, rows - 1, 0))
        two = jnp.where(
            row == rows - 1, second,
            jnp.where(row == rows - 2, first, pltpu.roll(wide, rows - 2, 0)),
        )
        return wide, one, two

    @pl.loop(0, slices)
    def _(j):
        cols = columns(j)
        k0, k1, k2 = advanced(kmg, cols, 0)
        kg_ref[:, cols] = (
            k0 * prm_ref[0:1, cols] + k1 * prm_ref[1:2, cols] + k2 * prm_ref[2:3, cols]
        ).astype(BF16)
        v0, v1, v2 = advanced(vmg, cols, 2)
        vg_ref[:, cols] = (
            v0 * prm_ref[3:4, cols] + v1 * prm_ref[4:5, cols] + v2 * prm_ref[5:6, cols]
        ).astype(BF16)

    @pl.loop(0, slices)
    def _(j):
        @pl.when(j != me)
        def _():
            to_ctx(
                total.at[j], total.at[j], send_sem.at[5, 0], recv_sem.at[5, j], j
            ).wait_recv()

        sum_ref[:, columns(j)] = total[j]

    @pl.when(me < n - 1)
    def _():
        tails.wait_send()

    @pl.when(me > 0)
    def _():
        heads.wait_send()

    for i in range(1, n_ch):
        to_ch(i).wait_send()
    sent(0, own, gathered, slices)
    sent(2, own_b, gathered_b, slices)
    sent(4, part, parts, slices)

    @pl.when(me < slices)
    def _():
        sent(1, prefix, incoming, n)
        sent(3, suffix, incoming_b, n)

        @pl.loop(0, n)
        def _(i):
            @pl.when(i != me)
            def _():
                to_ctx(
                    total.at[me], total.at[me], send_sem.at[5, i], recv_sem.at[5, me], i
                ).wait_send()


def local(
    query_proj, key_proj, value_proj, key_taps, value_taps,
    residues, decay_rates, skip_weight, norm_gain, out_grad,
):
    rows, channels = key_proj.shape
    groups, modes = residues.shape
    group_size = channels // groups
    n, n_ch = lax.axis_size("ctx"), lax.axis_size("ch")
    slices = channels // TILE
    assert modes == group_size and slices <= n and rows == 128
    key_spread = jnp.repeat(key_taps.astype(F32).T, group_size, axis=1)
    value_spread = jnp.repeat(value_taps.astype(F32).T, group_size, axis=1)
    params = jnp.concatenate(
        [
            key_spread, value_spread, skip_weight[None], norm_gain[None],
            decay_rates.reshape(1, channels), residues.reshape(1, channels),
            jnp.zeros((6, channels), F32),
        ],
        axis=0,
    )
    rate_rows = jnp.repeat(decay_rates.T, group_size, axis=1)
    positions = jnp.arange(rows).astype(F32)

    def lagged(places):
        return jnp.sum(
            residues[:, :, None] * jnp.exp(-decay_rates[:, :, None] * places[None, None, :]), axis=1
        )

    filt = lagged(positions)
    turned = lagged(jnp.where(positions > 0, rows - positions, 0.0))
    wide = jax.ShapeDtypeStruct((rows, channels), BF16)
    state = lambda count: pltpu.VMEM((count, group_size, TILE), F32)
    whole = lambda kind: pltpu.VMEM((rows, channels), kind)
    vmem = pl.BlockSpec(memory_space=pltpu.VMEM)
    mixed_out, query_grad, key_grad, value_grad, sums = pl.pallas_call(
        functools.partial(body, n, n_ch, slices, float(channels * n_ch), group_size),
        out_shape=(wide, wide, wide, wide, jax.ShapeDtypeStruct((8, channels), F32)),
        in_specs=[vmem] * 8,
        out_specs=(vmem,) * 5,
        scratch_shapes=[
            pltpu.VMEM((4, channels), F32), pltpu.VMEM((4, channels), F32),
            pltpu.VMEM((4, channels), F32), pltpu.VMEM((4, channels), F32),
            whole(BF16), whole(F32), whole(F32), whole(F32), whole(BF16), whole(BF16), whole(BF16),
            state(slices), state(n), state(n), state(slices),
            state(slices), state(n), state(n), state(slices),
            pltpu.VMEM((slices, 8, TILE), F32), pltpu.VMEM((n, 8, TILE), F32),
            pltpu.VMEM((slices, 8, TILE), F32),
            pltpu.VMEM((2, rows, 128), F32), pltpu.VMEM((rows, 128), F32),
            pltpu.VMEM((max(1, n_ch - 1), rows, 128), F32),
            pltpu.SemaphoreType.DMA((2,)), pltpu.SemaphoreType.DMA((2,)),
            pltpu.SemaphoreType.DMA((6, n)), pltpu.SemaphoreType.DMA((6, n)),
            pltpu.SemaphoreType.DMA((max(1, n_ch - 1),)), pltpu.SemaphoreType.DMA((max(1, n_ch - 1),)),
        ],
        compiler_params=pltpu.CompilerParams(
            collective_id=0, has_side_effects=True, vmem_limit_bytes=56 << 20
        ),
        name="hyena",
    )(query_proj, key_proj, value_proj, out_grad, params, rate_rows, filt, turned)
    taps = jnp.sum(sums[2:8].reshape(6, groups, group_size), axis=2)
    return (
        mixed_out, query_grad, key_grad, value_grad,
        taps[0:3].T, taps[3:6].T, sums[0], sums[1],
    )


def solution(mesh):
    wide = P("ctx", "ch")
    placed = (
        wide, wide, wide, P("ch", None), P("ch", None), P("ch", None), P("ch", None),
        P("ch"), P("ch"), wide,
    )
    return jax.shard_map(
        local, mesh=mesh, in_specs=placed,
        out_specs=(wide, wide, wide, wide, P("ch", None), P("ch", None), P("ch"), P("ch")),
        check_vma=False,
    )
```

time: 352 us -> 84.7 us (0.24); the launches traced: 346 us -> 84.3 us
  local copies, waits for them, and re-layouts: 120 us -> 15.2 us
  blocking collectives: 73.5 us -> 0 us
  Pallas kernels: 0 us -> 64.8 us
  other arithmetic: 47.6 us -> 3.5 us
  matrix products: 41.5 us -> 0 us
  waiting for transfers between devices: 38.1 us -> 0 us
  between operations: 15 us -> 0.83 us
  starting transfers between devices: 9.73 us -> 0 us
    gather x2 -> x0, local copies, waits for them, and re-layouts: 79.8 us -> none  [local(): filt_rows[:, jnp.clip(lag_index, 0, tok_rows - 1)]]
    psum x3 -> x0, blocking collectives: 73.5 us -> none  [the longest x1 62.2 us: local(): lax.psum((key_taps_part, value_taps_part, skip_part, gain_part), 'ctx')]
    pallas_call x0 -> x1, Pallas kernels: none -> 64.8 us  [local(): pl.pallas_call(functools.partial(body, n, n_ch, slices, float(channels *...]
    dot_general x6 -> x0, matrix products: 41.5 us -> none  [the longest x1 16.5 us: local(): jnp.einsum('gts,sgc->tgc', triangle, product_blocks, precision=HIGHEST)]
    all_gather x2 -> x0, waiting for transfers between devices: 38.1 us -> none  [the longest x1 38.1 us: local(): piece = lax.all_gather(own_begin[None], 'ctx', axis=0, tiled=True)]
    reduce_sum x11 -> x2, other arithmetic: 24.8 us -> 2.76 us  [the longest x1 2.49 us: lagged(): jnp.sum(residues[:, :, None] * jnp.exp(-decay_rates[:, :, None] * places[...]
    unnamed x51 -> x22, local copies, waits for them, and re-layouts: 24.7 us -> 6.26 us
    convert_element_type x9 -> x1, other arithmetic: 17.7 us -> 0.01 us  [local(): positions = jnp.arange(rows).astype(F32)]
  transfers between devices with their start and end apart: 6 -> 0, of which waited for: 1 -> 0; matrix products, arithmetic and copies ran while one was open for 39% -> 0% of each run, Pallas kernels for 0% -> 0%
where the time goes in v1:
time: 84.7 us; the launch traced here: 84.3 us
  Pallas kernels  64.8 us (77%)
  local copies, waits for them, and re-layouts  15.2 us (18%)
  other arithmetic  3.5 us (4%)
    pallas_call x1, Pallas kernels, local(): pl.pallas_call(functools.partial(body, n, n_ch, slices, float(channels *...  64.8 us
    unnamed x22, local copies, waits for them, and re-layouts  6.26 us
    reduce_sum x1, other arithmetic, lagged(): jnp.sum(residues[:, :, None] * jnp.exp(-decay_rates[:, :, None] * places[...  2.49 us
    reshape x1, local copies, waits for them, and re-layouts, local(): rate_rows = jnp.repeat(decay_rates.T, group_size, axis=1)  2.26 us

profile of v1, /device:TPU:0, one launch (start us, length us, event | category | flops | bytes accessed | tf_op | source)
XLA Modules:
  0.0 84.3 jit_solution(15153540499115997240)
XLA Ops:
  0.6 0.0 copy-start.3
  0.6 0.0 copy-start.6
  0.7 0.0 copy-start.7
  0.7 0.8 copy.27
  1.5 0.7 neg.5
  2.2 0.1 copy.29
  2.3 0.0 copy-start.4
  2.4 0.0 copy-start.5
  2.4 2.5 %multiply_reduce_fusion = (f32[256,128]{1,0:T(8,128)}, f32[256,128]{1,0:T(8,128)}) fusion(f32[128]{0:T(128)S(1)} %compare_select_fusion, f32[256,16]{1,0:T(8,128)S(1)} %copy.29, f32[256,16]{1,0:T(8,128)S(1)} %copy.27, f32[128]{0:T(128)S(1)} %iota_convert_fusion), kind=kLoop, calls=%fused_computation | loop fusion | flops 3080192 | bytes 295936 | tf_op jit(solution)/shard_map/reduce_sum | solution.py:427
  4.9 0.1 reshape.49
  5.0 0.0 copy-done.6
  5.0 0.2 broadcast_in_dim.26
  5.2 0.2 reshape.46
  5.4 0.0 copy-done.7
  5.4 0.2 broadcast_in_dim.27
  5.6 0.2 reshape.47
  5.8 0.0 copy-done.3
  5.8 0.1 copy.26
  5.9 0.1 reshape.48
  6.1 0.0 copy-done.4
  6.1 0.0 copy-done.5
  6.1 1.5 %concatenate.3.prm_ref = f32[16,4096]{1,0:T(8,128)} concatenate(f32[3,4096]{1,0:T(4,128)S(1)} %reshape.46, f32[3,4096]{1,0:T(4,128)S(1)} %reshape.47, f32[1,4096]{1,0:T(1,128)S(1)} %bitcast.14, f32[1,4096]{1,0:T(1,128)S(1)} %bitcast.15, f32[1,4096]{1,0:T(1,128)S(1)} %reshape.48, f32[1,4096]{1,0:T(1,128)S(1)} %reshape.49, f32[6,4096]{1,0:T(8,128)S(1)} %broadcast_in_dim.30), dimensions={0} | concatenate | bytes 524288 | tf_op jit(solution)/shard_map/concatenate | solution.py:415
  7.6 0.6 broadcast_in_dim.31
  8.2 2.3 %reshape.50.rate_ref = f32[16,4096]{1,0:T(8,128)} reshape(f32[16,256,16]{2,1,0:T(8,128)S(1)} %broadcast_in_dim.31) | data formatting | bytes 524288 | tf_op jit(solution)/shard_map/reshape | solution.py:423
  10.4 64.8 %hyena.1 = (bf16[128,4096]{1,0:T(8,128)(2,1)}, bf16[128,4096]{1,0:T(8,128)(2,1)}, bf16[128,4096]{1,0:T(8,128)(2,1)}, bf16[128,4096]{1,0:T(8,128)(2,1)}, f32[8,4096]{1,0:T(8,128)}) custom-call(bf16[128,4096]{1,0:T(8,128)(2,1)} %q_ref.1, bf16[128,4096]{1,0:T(8,128)(2,1)} %k_ref.1, bf16[128,4096]{1,0:T(8,128)(2,1)} %v_ref.1, bf16[128,4096]{1,0:T(8,128)(2,1)} %og_ref.1, ...), custom_call_target="tpu_custom_call" | custom-call | tf_op jit(solution)/shard_map/hyena/pallas_call | solution.py:437
  75.3 0.0 copy-start.2
  75.3 1.0 %slice.15 = f32[6,4096]{1,0:T(8,128)S(1)} slice(f32[8,4096]{1,0:T(8,128)} %get-tuple-element.17), slice={[2:8], [0:4096]} | slice | bytes 196608 | tf_op jit(solution)/shard_map/slice | solution.py:461
  76.3 0.3 reshape.51
  76.5 0.3 reduce_sum.29
  76.8 0.6 slice_bitcast_fusion
  77.4 1.6 %fusion = (f32[1,4096]{1,0:T(1,128)}, f32[1,4096]{1,0:T(1,128)}) fusion(f32[8,4096]{1,0:T(8,128)} %get-tuple-element.17), kind=kLoop, calls=%fused_computation.8 | loop fusion | bytes 65536 | tf_op jit(solution)/shard_map/slice | solution.py:464
  79.0 0.0 copy-start.1
  79.1 2.4 %copy.34 = bf16[128,4096]{1,0:T(8,128)(2,1)} copy(bf16[128,4096]{1,0:T(8,128)(2,1)} %get-tuple-element.32) | data formatting | bytes 2097152
  81.4 0.0 copy-done.2
  81.4 0.0 copy-start
  81.4 1.0 %copy.35 = bf16[128,4096]{1,0:T(8,128)(2,1)} copy(bf16[128,4096]{1,0:T(8,128)(2,1)S(1)} %copy-done.2) | data formatting | bytes 2097152
  82.4 0.0 copy-done.1
  82.4 1.0 %copy.36 = bf16[128,4096]{1,0:T(8,128)(2,1)} copy(bf16[128,4096]{1,0:T(8,128)(2,1)S(1)} %copy-done.1) | data formatting | bytes 2097152
  83.4 0.0 copy-done
  83.4 1.0 %copy.37 = bf16[128,4096]{1,0:T(8,128)(2,1)} copy(bf16[128,4096]{1,0:T(8,128)(2,1)S(1)} %copy-done) | data formatting | bytes 2097152
  (5 shorter events, 0.0 us)
Async XLA Ops:
  0.6 5.2 %copy-start.3 = (f32[256,16]{0,1:T(8,128)S(1)}, f32[256,16]{0,1:T(8,128)}, u32[]{:S(2)}) copy-start(f32[256,16]{0,1:T(8,128)} %param.16) | copy-start | bytes 49156
  0.6 4.3 %copy-start.6 = (bf16[256,3]{0,1:T(4,128)(2,1)S(1)}, bf16[256,3]{0,1:T(4,128)(2,1)}, u32[]{:S(2)}) copy-start(bf16[256,3]{0,1:T(4,128)(2,1)} %param.13) | copy-start | bytes 4612
  0.7 4.7 %copy-start.7 = (bf16[256,3]{0,1:T(4,128)(2,1)S(1)}, bf16[256,3]{0,1:T(4,128)(2,1)}, u32[]{:S(2)}) copy-start(bf16[256,3]{0,1:T(4,128)(2,1)} %param.14) | copy-start | bytes 4612
  2.3 3.7 %copy-start.4 = (f32[4096]{0:T(1024)S(1)}, f32[4096]{0:T(1024)}, u32[]{:S(2)}) copy-start(f32[4096]{0:T(1024)} %param.17) | copy-start | bytes 49156
  2.4 3.7 %copy-start.5 = (f32[4096]{0:T(1024)S(1)}, f32[4096]{0:T(1024)}, u32[]{:S(2)}) copy-start(f32[4096]{0:T(1024)} %param.18) | copy-start | bytes 49156
  75.3 6.2 %copy-start.2 = (bf16[128,4096]{1,0:T(8,128)(2,1)S(1)}, bf16[128,4096]{1,0:T(8,128)(2,1)}, u32[]{:S(2)}) copy-start(bf16[128,4096]{1,0:T(8,128)(2,1)} %get-tuple-element.33) | copy-start | bytes 3145732
  79.0 3.4 %copy-start.1 = (bf16[128,4096]{1,0:T(8,128)(2,1)S(1)}, bf16[128,4096]{1,0:T(8,128)(2,1)}, u32[]{:S(2)}) copy-start(bf16[128,4096]{1,0:T(8,128)(2,1)} %get-tuple-element.34) | copy-start | bytes 3145732
  81.4 1.9 %copy-start = (bf16[128,4096]{1,0:T(8,128)(2,1)S(1)}, bf16[128,4096]{1,0:T(8,128)(2,1)}, u32[]{:S(2)}) copy-start(bf16[128,4096]{1,0:T(8,128)(2,1)} %get-tuple-element.35) | copy-start | bytes 3145732

commit v2 on v1

v2 whole, which is shorter than its diff:
```python
import functools

import jax
import jax.numpy as jnp
from jax import lax
from jax.experimental import pallas as pl
from jax.experimental.pallas import tpu as pltpu
from jax.sharding import PartitionSpec as P

EPSILON = 1e-06
TILE = 256
CHUNK = 32
HIGHEST = lax.Precision.HIGHEST
F32, BF16 = jnp.float32, jnp.bfloat16


def halves(wide):
    high = wide.astype(BF16)
    return high, (wide - high.astype(F32)).astype(BF16)


def contract_rows(weights, signal):
    return lax.dot_general(weights, signal, (((0,), (0,)), ((), ())), preferred_element_type=F32)


def body(
    n, n_ch, slices, width_all, group_size,
    q_ref, k_ref, v_ref, kt_ref, vt_ref, res_ref, rates_ref, skip_ref, gain_ref, og_ref,
    out_ref, qg_ref, kg_ref, vg_ref, ktg_ref, vtg_ref, skg_ref, gng_ref,
    tail_out, tail_in, head_out, head_in, before, last, taps,
    lag_up, lag_down, filt, turned,
    prod, kmix, vmix, mixed, mgrad,
    own, gathered, prefix, incoming,
    own_b, gathered_b, suffix, incoming_b,
    part, parts, total,
    row_acc, row_out, row_in,
    tail_sem, head_sem, send_sem, recv_sem, ch_send, ch_recv,
):
    me = lax.axis_index("ctx")
    me_ch = lax.axis_index("ch")
    rows = q_ref.shape[0]

    def to_ctx(src, dst, s_sem, r_sem, peer):
        return pltpu.make_async_remote_copy(
            src_ref=src, dst_ref=dst, send_sem=s_sem, recv_sem=r_sem,
            device_id={"ctx": peer}, device_id_type=pl.DeviceIdType.MESH,
        )

    def columns(j):
        return pl.ds(pl.multiple_of(j * TILE, TILE), TILE)

    barrier = pltpu.get_barrier_semaphore()

    @pl.loop(1, n)
    def _(i):
        pl.semaphore_signal(
            barrier, inc=1, device_id={"ctx": lax.rem(me + i, n)},
            device_id_type=pl.DeviceIdType.MESH,
        )

    for i in range(1, n_ch):
        pl.semaphore_signal(
            barrier, inc=1, device_id={"ch": lax.rem(me_ch + i, n_ch)},
            device_id_type=pl.DeviceIdType.MESH,
        )
    tail_out[0:2] = k_ref[rows - 16 : rows].astype(F32)[14:16]
    tail_out[2:4] = v_ref[rows - 16 : rows].astype(F32)[14:16]
    groups_tile = TILE // group_size
    row_wide = lax.broadcasted_iota(jnp.int32, (rows, TILE), 0).astype(F32)
    lane_group = lax.broadcasted_iota(jnp.int32, (CHUNK, TILE), 1) // group_size
    member = (
        lax.broadcasted_iota(jnp.int32, (groups_tile, TILE), 0)
        == lax.broadcasted_iota(jnp.int32, (groups_tile, TILE), 1) // group_size
    )
    member_wide = member.astype(F32)
    repeat_wide = (
        lax.broadcasted_iota(jnp.int32, (group_size, TILE), 0)
        == lax.rem(lax.broadcasted_iota(jnp.int32, (group_size, TILE), 1), group_size)
    ).astype(F32)
    block_mask = (
        lax.broadcasted_iota(jnp.int32, (TILE, TILE), 0) // group_size
        == lax.broadcasted_iota(jnp.int32, (TILE, TILE), 1) // group_size
    )
    tri_row = lax.broadcasted_iota(jnp.int32, (rows, rows), 0)
    tri_col = lax.broadcasted_iota(jnp.int32, (rows, rows), 1)

    def group_rows(j):
        return pl.ds(pl.multiple_of(j * groups_tile, groups_tile), groups_tile)

    def over_channels(table):
        return lax.dot_general(
            table, member_wide, (((0,), (0,)), ((), ())),
            precision=HIGHEST, preferred_element_type=F32,
        )

    def as_line(table):
        wide = jnp.dot(table, repeat_wide, precision=HIGHEST, preferred_element_type=F32)
        return jnp.sum(jnp.where(member, wide, 0.0), axis=0, keepdims=True)

    @pl.loop(0, slices)
    def _(j):
        cols, lines = columns(j), group_rows(j)
        taps[0:3, cols] = over_channels(kt_ref[lines, :].astype(F32))
        taps[3:6, cols] = over_channels(vt_ref[lines, :].astype(F32))
        rate_line = as_line(rates_ref[lines, :])
        a_high, a_low = halves(jnp.where(member, as_line(res_ref[lines, :]), 0.0))
        weights = jnp.concatenate([a_high, a_high, a_low], axis=1)
        for table, filter_rows, lag in (
            (lag_up, filt, row_wide), (lag_down, turned, rows - 1.0 - row_wide)
        ):
            high, low = halves(jnp.exp(-rate_line * lag))
            table[0:rows, cols] = high
            table[rows : 2 * rows, cols] = low
            filter_rows[lines, :] = lax.dot_general(
                weights, jnp.concatenate([high, low, high], axis=1),
                (((1,), (1,)), ((), ())), preferred_element_type=F32,
            )

    pl.semaphore_wait(barrier, n - 1 + n_ch - 1)

    tails = to_ctx(tail_out, tail_in, tail_sem.at[0], tail_sem.at[1], lax.rem(me + 1, n))
    heads = to_ctx(head_out, head_in, head_sem.at[0], head_sem.at[1], lax.rem(me + n - 1, n))

    @pl.when(me < n - 1)
    def _():
        tails.start()

    @pl.when(me == 0)
    def _():
        tail_in[...] = jnp.zeros(tail_in.shape, F32)

    @pl.when(me > 0)
    def _():
        tails.wait_recv()

    before[0, 14:16] = tail_in[0:2]
    before[1, 14:16] = tail_in[2:4]

    def delayed(ref, cols, which, r):
        if r == 0:
            wide = jnp.concatenate([before[which, :, cols], ref[0:CHUNK, cols].astype(F32)], axis=0)
        else:
            wide = ref[r - 16 : r + CHUNK, cols].astype(F32)
        return wide[16 : 16 + CHUNK], wide[15 : 15 + CHUNK], wide[14 : 14 + CHUNK]

    def mix(parts_of, cols, base):
        zero, one, two = parts_of
        return (
            zero * taps[base : base + 1, cols]
            + one * taps[base + 1 : base + 2, cols]
            + two * taps[base + 2 : base + 3, cols]
        )

    def folded(x):
        return jnp.sum(x.reshape(x.shape[0] // 8, 8, TILE), axis=0)

    def modal(table, cols, signal):
        full = contract_rows(table[:, cols], jnp.concatenate([signal, signal], axis=0))
        kept = jnp.where(block_mask, full, 0.0)
        return jnp.sum(kept.reshape(groups_tile, group_size, TILE), axis=0)

    def spread(table, cols, state):
        high, low = table[0:rows, cols], table[rows : 2 * rows, cols]
        s_high, s_low = halves(state)
        zero = jnp.zeros((TILE, TILE), F32)
        big = [
            jnp.where(block_mask, jnp.concatenate([x.astype(F32)] * groups_tile, axis=0), zero)
            .astype(BF16)
            for x in (s_high, s_low)
        ]
        return jnp.dot(
            jnp.concatenate([high, low, high], axis=1),
            jnp.concatenate([big[0], big[0], big[1]], axis=0),
            preferred_element_type=F32,
        )

    def toeplitz(table, shift, j, ref, cols, keep):
        lines = table[group_rows(j), :]
        lhs, rhs = [], []
        for g in range(groups_tile):
            spread_line = jnp.broadcast_to(lines[g : g + 1, :], (rows, rows))
            turned_line = pltpu.roll(spread_line, shift, 1, stride=1, stride_axis=0)
            lhs.append(jnp.where(keep, turned_line, 0.0).astype(BF16))
            for r in range(0, rows, CHUNK):
                wide = ref[r : r + CHUNK, cols].astype(F32)
                rhs.append(jnp.where(lane_group == g, wide, 0.0).astype(BF16))
        return jnp.dot(
            jnp.concatenate(lhs, axis=1), jnp.concatenate(rhs, axis=0),
            preferred_element_type=F32,
        )

    def scatter(phase, source, target, j):
        copy = to_ctx(
            source.at[j], target.at[me], send_sem.at[phase, j], recv_sem.at[phase, me], j
        )

        @pl.when(j != me)
        def _():
            copy.start()

        @pl.when(j == me)
        def _():
            target[me] = source[j]

    def arrive(phase, source, target, i):
        @pl.when(i != me)
        def _():
            to_ctx(
                source.at[0], target.at[i], send_sem.at[phase, 0], recv_sem.at[phase, i], i
            ).wait_recv()

    def sent(phase, source, target, count):
        @pl.loop(0, count)
        def _(j):
            @pl.when(j != me)
            def _():
                to_ctx(
                    source.at[j], target.at[me], send_sem.at[phase, j], recv_sem.at[phase, me], j
                ).wait_send()

    @pl.loop(0, slices)
    def _(i):
        j = lax.rem(me + i, slices)
        cols = columns(j)
        for r in range(0, rows, CHUNK):
            part_rows = slice(r, r + CHUNK)
            key = mix(delayed(k_ref, cols, 0, r), cols, 0)
            value = mix(delayed(v_ref, cols, 1, r), cols, 3)
            kmix[part_rows, cols] = key
            vmix[part_rows, cols] = value
            prod[part_rows, cols] = (key * value).astype(BF16)
        own[j] = modal(lag_down, cols, prod[:, cols])
        scatter(0, own, gathered, j)

    def long_forward(j):
        cols = columns(j)
        mixed[:, cols] = toeplitz(turned, 1, j, prod, cols, tri_row >= tri_col)

    early = slices // 2

    @pl.loop(0, early)
    def _(j):
        long_forward(j)

    @pl.when(me < slices)
    def _():
        rate_here = over_channels(rates_ref[group_rows(me), :])
        fall = jnp.exp(-rate_here * float(rows))
        scale = over_channels(res_ref[group_rows(me), :]) * jnp.exp(-rate_here)

        def step(i, carry):
            prefix[i] = carry * scale
            scatter(1, prefix, incoming, i)
            arrive(0, own, gathered, i)
            return fall * carry + gathered[i]

        lax.fori_loop(0, n, step, jnp.zeros((group_size, TILE), F32))

    @pl.loop(early, slices)
    def _(j):
        long_forward(j)

    row_acc[...] = jnp.zeros(row_acc.shape, F32)

    @pl.loop(0, slices)
    def _(i):
        j = lax.rem(me + i, slices)
        cols = columns(j)
        arrive(1, prefix, incoming, j)
        mixed[:, cols] += spread(lag_up, cols, incoming[j])
        for r in range(0, rows, CHUNK):
            part_rows = slice(r, r + CHUNK)
            full = mixed[part_rows, cols] + skip_ref[0:1, cols] * prod[part_rows, cols].astype(F32)
            mixed[part_rows, cols] = full
            gated = q_ref[part_rows, cols].astype(F32) * full
            squares = gated * gated
            along = gated * gain_ref[0:1, cols] * og_ref[part_rows, cols].astype(F32)
            row_acc[0, part_rows] += squares[:, :128] + squares[:, 128:]
            row_acc[1, part_rows] += along[:, :128] + along[:, 128:]

    lane = lax.broadcasted_iota(jnp.int32, (rows, 128), 1)
    squares = jnp.sum(row_acc[0], axis=1, keepdims=True)
    along = jnp.sum(row_acc[1], axis=1, keepdims=True)
    row_out[...] = jnp.where(lane == 0, squares, along)

    def to_ch(i):
        return pltpu.make_async_remote_copy(
            src_ref=row_out, dst_ref=row_in.at[i - 1], send_sem=ch_send.at[i - 1],
            recv_sem=ch_recv.at[i - 1], device_id={"ch": lax.rem(me_ch + i, n_ch)},
            device_id_type=pl.DeviceIdType.MESH,
        )

    for i in range(1, n_ch):
        to_ch(i).start()
    summed = row_out[...]
    for i in range(1, n_ch):
        to_ch(i).wait_recv()
        summed = summed + row_in[i - 1]
    squares, along = summed[:, 0:1], summed[:, 1:2]
    scaled = lax.rsqrt(squares / width_all + EPSILON)
    pull = scaled * scaled * scaled * along / width_all
    row_acc[0] = jnp.broadcast_to(scaled, (rows, 128))
    row_acc[1] = jnp.broadcast_to(pull, (rows, 128))

    @pl.loop(0, slices)
    def _(i):
        j = lax.rem(me + i, slices)
        cols = columns(j)
        gain = gain_ref[0:1, cols]
        skip_sum = gain_sum = jnp.zeros((8, TILE), F32)
        for r in range(0, rows, CHUNK):
            part_rows = slice(r, r + CHUNK)
            scaled = jnp.concatenate([row_acc[0, part_rows]] * 2, axis=1)
            pull = jnp.concatenate([row_acc[1, part_rows]] * 2, axis=1)
            query = q_ref[part_rows, cols].astype(F32)
            grad = og_ref[part_rows, cols].astype(F32)
            full = mixed[part_rows, cols]
            gated = query * full
            normed = gated * scaled
            out_ref[part_rows, cols] = (normed * gain).astype(BF16)
            gated_grad = scaled * gain * grad - gated * pull
            qg_ref[part_rows, cols] = (gated_grad * full).astype(BF16)
            mixed_grad = (gated_grad * query).astype(BF16)
            mgrad[part_rows, cols] = mixed_grad
            skip_sum += folded(mixed_grad.astype(F32) * prod[part_rows, cols].astype(F32))
            gain_sum += folded(grad * normed)
        part[j, 0:1, :] = jnp.sum(skip_sum, axis=0, keepdims=True)
        part[j, 1:2, :] = jnp.sum(gain_sum, axis=0, keepdims=True)
        own_b[j] = modal(lag_up, cols, mgrad[:, cols])
        scatter(2, own_b, gathered_b, j)

    def long_backward(j):
        cols = columns(j)
        mixed[:, cols] = toeplitz(filt, 0, j, mgrad, cols, tri_row <= tri_col)

    @pl.loop(0, early)
    def _(j):
        long_backward(j)

    @pl.when(me < slices)
    def _():
        rate_here = over_channels(rates_ref[group_rows(me), :])
        fall = jnp.exp(-rate_here * float(rows))
        scale = over_channels(res_ref[group_rows(me), :]) * jnp.exp(-rate_here)

        def step(i, carry):
            place = n - 1 - i
            suffix[place] = carry * scale
            scatter(3, suffix, incoming_b, place)
            arrive(2, own_b, gathered_b, place)
            return fall * carry + gathered_b[place]

        lax.fori_loop(0, n, step, jnp.zeros((group_size, TILE), F32))

    @pl.loop(early, slices)
    def _(j):
        long_backward(j)

    @pl.loop(0, slices)
    def _(i):
        j = lax.rem(me + i, slices)
        cols = columns(j)
        arrive(3, suffix, incoming_b, j)
        mixed[:, cols] += spread(lag_down, cols, incoming_b[j])
        sums = [jnp.zeros((8, TILE), F32)] * 6
        later = [jnp.zeros((8, TILE), F32)] * 2
        for r in reversed(range(0, rows, CHUNK)):
            part_rows = slice(r, r + CHUNK)
            pgrad = (
                mixed[part_rows, cols] + skip_ref[0:1, cols] * mgrad[part_rows, cols].astype(F32)
            )
            for which, (other, signal, target) in enumerate(
                ((vmix, k_ref, kg_ref), (kmix, v_ref, vg_ref))
            ):
                zero = (pgrad * other[part_rows, cols]).astype(BF16).astype(F32)
                wide = jnp.concatenate([zero, later[which]], axis=0)
                shifted = (zero, wide[1 : 1 + CHUNK], wide[2 : 2 + CHUNK])
                later[which] = zero[0:8]
                target[part_rows, cols] = mix(shifted, cols, 3 * which).astype(BF16)
                inside = signal[part_rows, cols].astype(F32)
                for offset in range(3):
                    place = 3 * which + offset
                    sums[place] = sums[place] + folded(shifted[offset] * inside)
                if r == rows - CHUNK:
                    last[which, 0:16, cols] = zero[CHUNK - 16 :]
        for which in range(2):
            first, second = later[which][0:1], later[which][1:2]
            head_out[2 * which : 2 * which + 2, cols] = later[which][0:2]
            older = tail_in[2 * which : 2 * which + 1, cols]
            newer = tail_in[2 * which + 1 : 2 * which + 2, cols]
            edges = (0.0, first * newer, first * older + second * newer)
            for offset in range(3):
                place = 3 * which + offset
                part[j, 2 + place : 3 + place, :] = (
                    jnp.sum(sums[place], axis=0, keepdims=True) + edges[offset]
                )
        scatter(4, part, parts, j)

    @pl.when(me > 0)
    def _():
        heads.start()

    @pl.when(me == n - 1)
    def _():
        head_in[...] = jnp.zeros(head_in.shape, F32)

    @pl.when(me < slices)
    def _():
        def step(i, carry):
            arrive(4, part, parts, i)
            return carry + parts[i]

        total[me] = lax.fori_loop(0, n, step, jnp.zeros((8, TILE), F32))

        @pl.loop(0, n)
        def _(i):
            @pl.when(i != me)
            def _():
                to_ctx(
                    total.at[me], total.at[me], send_sem.at[5, i], recv_sem.at[5, me], i
                ).start()

    @pl.when(me < n - 1)
    def _():
        heads.wait_recv()

    last[0, 16:18] = head_in[0:2]
    last[1, 16:18] = head_in[2:4]

    @pl.loop(0, slices)
    def _(j):
        cols = columns(j)
        for which, target in ((0, kg_ref), (1, vg_ref)):
            wide = last[which, :, cols]
            shifted = (wide[0:16], wide[1:17], wide[2:18])
            target[rows - 16 : rows, cols] = mix(shifted, cols, 3 * which).astype(BF16)

    @pl.loop(0, slices)
    def _(j):
        @pl.when(j != me)
        def _():
            to_ctx(
                total.at[j], total.at[j], send_sem.at[5, 0], recv_sem.at[5, j], j
            ).wait_recv()

        cols, lines = columns(j), group_rows(j)
        here = total[j]
        skg_ref[0:1, cols] = here[0:1]
        gng_ref[0:1, cols] = here[1:2]
        by_group = lax.dot_general(
            member_wide, here, (((1,), (1,)), ((), ())),
            precision=HIGHEST, preferred_element_type=F32,
        )
        ktg_ref[lines, :] = by_group[:, 2:5]
        vtg_ref[lines, :] = by_group[:, 5:8]

    @pl.when(me < n - 1)
    def _():
        tails.wait_send()

    @pl.when(me > 0)
    def _():
        heads.wait_send()

    for i in range(1, n_ch):
        to_ch(i).wait_send()
    sent(0, own, gathered, slices)
    sent(2, own_b, gathered_b, slices)
    sent(4, part, parts, slices)

    @pl.when(me < slices)
    def _():
        sent(1, prefix, incoming, n)
        sent(3, suffix, incoming_b, n)

        @pl.loop(0, n)
        def _(i):
            @pl.when(i != me)
            def _():
                to_ctx(
                    total.at[me], total.at[me], send_sem.at[5, i], recv_sem.at[5, me], i
                ).wait_send()


def local(
    query_proj, key_proj, value_proj, key_taps, value_taps,
    residues, decay_rates, skip_weight, norm_gain, out_grad,
):
    rows, channels = key_proj.shape
    groups, modes = residues.shape
    group_size = channels // groups
    n, n_ch = lax.axis_size("ctx"), lax.axis_size("ch")
    slices = channels // TILE
    assert modes == group_size and slices <= n and rows == 128
    wide = jax.ShapeDtypeStruct((rows, channels), BF16)
    state = lambda count: pltpu.VMEM((count, group_size, TILE), F32)
    whole = lambda kind: pltpu.VMEM((rows, channels), kind)
    vmem = pl.BlockSpec(memory_space=pltpu.VMEM)
    taps_shape = jax.ShapeDtypeStruct(key_taps.shape, F32)
    line_shape = jax.ShapeDtypeStruct((1, channels), F32)
    *results, skip_grad, gain_grad = pl.pallas_call(
        functools.partial(body, n, n_ch, slices, float(channels * n_ch), group_size),
        out_shape=(wide,) * 4 + (taps_shape,) * 2 + (line_shape,) * 2,
        in_specs=[vmem] * 10,
        out_specs=(vmem,) * 8,
        scratch_shapes=[
            pltpu.VMEM((4, channels), F32), pltpu.VMEM((4, channels), F32),
            pltpu.VMEM((4, channels), F32), pltpu.VMEM((4, channels), F32),
            pltpu.VMEM((2, 16, channels), F32), pltpu.VMEM((2, 24, channels), F32),
            pltpu.VMEM((8, channels), F32),
            pltpu.VMEM((2 * rows, channels), BF16), pltpu.VMEM((2 * rows, channels), BF16),
            pltpu.VMEM((groups, rows), F32), pltpu.VMEM((groups, rows), F32),
            whole(BF16), whole(F32), whole(F32), whole(F32), whole(BF16),
            state(slices), state(n), state(n), state(slices),
            state(slices), state(n), state(n), state(slices),
            pltpu.VMEM((slices, 8, TILE), F32), pltpu.VMEM((n, 8, TILE), F32),
            pltpu.VMEM((slices, 8, TILE), F32),
            pltpu.VMEM((2, rows, 128), F32), pltpu.VMEM((rows, 128), F32),
            pltpu.VMEM((max(1, n_ch - 1), rows, 128), F32),
            pltpu.SemaphoreType.DMA((2,)), pltpu.SemaphoreType.DMA((2,)),
            pltpu.SemaphoreType.DMA((6, n)), pltpu.SemaphoreType.DMA((6, n)),
            pltpu.SemaphoreType.DMA((max(1, n_ch - 1),)), pltpu.SemaphoreType.DMA((max(1, n_ch - 1),)),
        ],
        compiler_params=pltpu.CompilerParams(
            collective_id=0, has_side_effects=True, vmem_limit_bytes=56 << 20
        ),
        name="hyena",
    )(
        query_proj, key_proj, value_proj, key_taps, value_taps, residues, decay_rates,
        skip_weight.reshape(1, channels), norm_gain.reshape(1, channels), out_grad,
    )
    return (*results, skip_grad.reshape(channels), gain_grad.reshape(channels))


def solution(mesh):
    wide = P("ctx", "ch")
    placed = (
        wide, wide, wide, P("ch", None), P("ch", None), P("ch", None), P("ch", None),
        P("ch"), P("ch"), wide,
    )
    return jax.shard_map(
        local, mesh=mesh, in_specs=placed,
        out_specs=(wide, wide, wide, wide, P("ch", None), P("ch", None), P("ch"), P("ch")),
        check_vma=False,
    )
```

time: 84.7 us -> 86.7 us (1.024); the launches traced: 84.3 us -> 85.3 us
  Pallas kernels: 64.8 us -> 70.8 us
  other arithmetic: 3.5 us -> 0 us
  local copies, waits for them, and re-layouts: 15.2 us -> 13.9 us
    unnamed x22 -> x32, local copies, waits for them, and re-layouts: 6.26 us -> 13.9 us
    pallas_call x1, Pallas kernels: 64.8 us -> 70.8 us  [local(): pl.pallas_call(functools.partial(body, n, n_ch, slices, float(channels *...]
    reshape x6 -> x0, local copies, waits for them, and re-layouts: 3.22 us -> none  [the longest x1 2.26 us: local(): rate_rows = jnp.repeat(decay_rates.T, group_size, axis=1)]
    reduce_sum x2 -> x0, other arithmetic: 2.76 us -> none  [the longest x1 2.49 us: lagged(): jnp.sum(residues[:, :, None] * jnp.exp(-decay_rates[:, :, None] * places[...]
    slice x2 -> x0, local copies, waits for them, and re-layouts: 2.62 us -> none  [the longest x1 1.61 us: local(): sums[1]]
    concatenate x1 -> x0, local copies, waits for them, and re-layouts: 1.47 us -> none  [local(): jnp.concatenate([key_spread, value_spread, skip_weight[None], norm_gain[N...]
    broadcast_in_dim x4 -> x0, local copies, waits for them, and re-layouts: 0.92 us -> none  [the longest x1 0.6 us: local(): rate_rows = jnp.repeat(decay_rates.T, group_size, axis=1)]
where the time goes in v2:
time: 86.7 us; the launch traced here: 85.3 us
  Pallas kernels  70.8 us (82%)
  local copies, waits for them, and re-layouts  13.9 us (16%)
    pallas_call x1, Pallas kernels, local(): pl.pallas_call(functools.partial(body, n, n_ch, slices, float(channels *...  70.8 us
    unnamed x32, local copies, waits for them, and re-layouts  13.9 us

profile of v2, /device:TPU:0, one launch (start us, length us, event | category | flops | bytes accessed | tf_op | source)
XLA Modules:
  0.0 85.3 jit_solution(10587904624776609151)
XLA Ops:
  0.6 0.0 copy-start.8
  0.6 0.7 copy-done.8
  1.3 0.0 copy-start.9
  1.3 0.8 copy.18.kt_ref
  2.1 0.0 copy-done.9
  2.1 0.0 copy-start.4
  2.1 0.8 copy.19.vt_ref
  2.8 0.0 copy-done.4
  2.8 0.0 copy-start.5
  2.8 0.8 copy.20.res_ref
  3.6 0.0 copy-done.5
  3.6 0.8 copy.21.rates_ref
  4.4 70.8 %hyena.1 = (bf16[128,4096]{1,0:T(8,128)(2,1)}, bf16[128,4096]{1,0:T(8,128)(2,1)}, bf16[128,4096]{1,0:T(8,128)(2,1)}, bf16[128,4096]{1,0:T(8,128)(2,1)}, f32[256,...) custom-call(bf16[128,4096]{1,0:T(8,128)(2,1)} %q_ref.1, bf16[128,4096]{1,0:T(8,128)(2,1)} %k_ref.1, ...), custom_call_target="tpu_custom_call" | custom-call | tf_op jit(solution)/shard_map/hyena/pallas_call | solution.py:501
  75.1 0.0 copy-start.3
  75.1 1.6 %copy.22 = f32[256,3]{0,1:T(4,128)} copy(f32[256,3]{1,0:T(8,128)} %get-tuple-element.28) | data formatting | bytes 6144
  76.7 0.0 copy-done.3
  76.7 0.7 copy.23
  77.4 0.0 copy-start.2
  77.4 2.4 %copy.30 = bf16[128,4096]{1,0:T(8,128)(2,1)} copy(bf16[128,4096]{1,0:T(8,128)(2,1)} %get-tuple-element.40) | data formatting | bytes 2097152
  79.8 0.0 copy-done.2
  79.8 0.0 copy-start.1
  79.8 1.0 %copy.31 = bf16[128,4096]{1,0:T(8,128)(2,1)} copy(bf16[128,4096]{1,0:T(8,128)(2,1)S(1)} %copy-done.2) | data formatting | bytes 2097152
  80.8 0.6 copy-done.1
  81.4 0.0 copy-start
  81.4 1.0 %copy.32 = bf16[128,4096]{1,0:T(8,128)(2,1)} copy(bf16[128,4096]{1,0:T(8,128)(2,1)S(1)} %copy-done.1) | data formatting | bytes 2097152
  82.4 0.6 copy-done
  83.0 0.0 copy-start.7
  83.0 1.0 %copy.33 = bf16[128,4096]{1,0:T(8,128)(2,1)} copy(bf16[128,4096]{1,0:T(8,128)(2,1)S(1)} %copy-done) | data formatting | bytes 2097152
  84.0 0.0 copy-done.7
  84.0 0.0 copy-start.6
  84.0 0.6 copy.34
  84.6 0.1 copy-done.6
  84.7 0.6 copy.35
Async XLA Ops:
  0.6 0.7 copy-start.8
  1.3 0.8 copy-start.9
  2.1 0.8 copy-start.4
  2.8 0.8 copy-start.5
  75.1 1.6 %copy-start.3 = (f32[256,3]{1,0:T(8,128)S(1)}, f32[256,3]{1,0:T(8,128)}, u32[]{:S(2)}) copy-start(f32[256,3]{1,0:T(8,128)} %get-tuple-element.29) | copy-start | bytes 9220
  77.4 2.4 %copy-start.2 = (bf16[128,4096]{1,0:T(8,128)(2,1)S(1)}, bf16[128,4096]{1,0:T(8,128)(2,1)}, u32[]{:S(2)}) copy-start(bf16[128,4096]{1,0:T(8,128)(2,1)} %get-tuple-element.41) | copy-start | bytes 3145732
  79.8 1.6 %copy-start.1 = (bf16[128,4096]{1,0:T(8,128)(2,1)S(1)}, bf16[128,4096]{1,0:T(8,128)(2,1)}, u32[]{:S(2)}) copy-start(bf16[128,4096]{1,0:T(8,128)(2,1)} %get-tuple-element.42) | copy-start | bytes 3145732
  81.4 1.6 %copy-start = (bf16[128,4096]{1,0:T(8,128)(2,1)S(1)}, bf16[128,4096]{1,0:T(8,128)(2,1)}, u32[]{:S(2)}) copy-start(bf16[128,4096]{1,0:T(8,128)(2,1)} %get-tuple-element.43) | copy-start | bytes 3145732
  83.0 1.0 %copy-start.7 = (f32[1,4096]{1,0:T(1,128)S(1)}, f32[1,4096]{1,0:T(1,128)}, u32[]{:S(2)}) copy-start(f32[1,4096]{1,0:T(1,128)} %get-tuple-element.22) | copy-start | bytes 49156
  84.0 0.7 copy-start.6

commit v3 on v2

--- a/solution.py
+++ b/solution.py
@@ -25,8 +25,9 @@
 
 def body(
     n, n_ch, slices, width_all, group_size,
-    q_ref, k_ref, v_ref, kt_ref, vt_ref, res_ref, rates_ref, skip_ref, gain_ref, og_ref,
-    out_ref, qg_ref, kg_ref, vg_ref, ktg_ref, vtg_ref, skg_ref, gng_ref,
+    q_hbm, k_hbm, v_hbm, kt_ref, vt_ref, res_ref, rates_ref, skip_ref, gain_ref, og_hbm,
+    out_hbm, qg_hbm, kg_hbm, vg_hbm, ktg_ref, vtg_ref, skg_ref, gng_ref,
+    q_ref, k_ref, v_ref, og_ref, out_ref, qg_ref, kg_ref, vg_ref, io_sem, by_group,
     tail_out, tail_in, head_out, head_in, before, last, taps,
     lag_up, lag_down, filt, turned,
     prod, kmix, vmix, mixed, mgrad,
@@ -39,6 +40,18 @@
     me = lax.axis_index("ctx")
     me_ch = lax.axis_index("ch")
     rows = q_ref.shape[0]
+    load_k, load_v, load_q, load_og = (
+        pltpu.make_async_copy(src, dst, io_sem.at[place])
+        for place, (src, dst) in enumerate(
+            ((k_hbm, k_ref), (v_hbm, v_ref), (q_hbm, q_ref), (og_hbm, og_ref))
+        )
+    )
+    stores = [
+        pltpu.make_async_copy(src, dst, io_sem.at[4 + place])
+        for place, (src, dst) in enumerate(
+            ((out_ref, out_hbm), (qg_ref, qg_hbm), (kg_ref, kg_hbm), (vg_ref, vg_hbm))
+        )
+    ]
 
     def to_ctx(src, dst, s_sem, r_sem, peer):
         return pltpu.make_async_remote_copy(
@@ -63,6 +76,10 @@
             barrier, inc=1, device_id={"ch": lax.rem(me_ch + i, n_ch)},
             device_id_type=pl.DeviceIdType.MESH,
         )
+    for load in (load_k, load_v, load_q, load_og):
+        load.start()
+    load_k.wait()
+    load_v.wait()
     tail_out[0:2] = k_ref[rows - 16 : rows].astype(F32)[14:16]
     tail_out[2:4] = v_ref[rows - 16 : rows].astype(F32)[14:16]
     groups_tile = TILE // group_size
@@ -72,11 +89,6 @@
         lax.broadcasted_iota(jnp.int32, (groups_tile, TILE), 0)
         == lax.broadcasted_iota(jnp.int32, (groups_tile, TILE), 1) // group_size
     )
-    member_wide = member.astype(F32)
-    repeat_wide = (
-        lax.broadcasted_iota(jnp.int32, (group_size, TILE), 0)
-        == lax.rem(lax.broadcasted_iota(jnp.int32, (group_size, TILE), 1), group_size)
-    ).astype(F32)
     block_mask = (
         lax.broadcasted_iota(jnp.int32, (TILE, TILE), 0) // group_size
         == lax.broadcasted_iota(jnp.int32, (TILE, TILE), 1) // group_size
@@ -84,26 +96,37 @@
     tri_row = lax.broadcasted_iota(jnp.int32, (rows, rows), 0)
     tri_col = lax.broadcasted_iota(jnp.int32, (rows, rows), 1)
 
+    groups = rates_ref.shape[1]
+    own_lane = (
+        lax.broadcasted_iota(jnp.int32, (group_size, TILE), 0)
+        == lax.rem(lax.broadcasted_iota(jnp.int32, (group_size, TILE), 1), group_size)
+    )
+
     def group_rows(j):
         return pl.ds(pl.multiple_of(j * groups_tile, groups_tile), groups_tile)
 
-    def over_channels(table):
-        return lax.dot_general(
-            table, member_wide, (((0,), (0,)), ((), ())),
-            precision=HIGHEST, preferred_element_type=F32,
-        )
-
-    def as_line(table):
-        wide = jnp.dot(table, repeat_wide, precision=HIGHEST, preferred_element_type=F32)
-        return jnp.sum(jnp.where(member, wide, 0.0), axis=0, keepdims=True)
+    def holds(j):
+        group = lax.broadcasted_iota(jnp.int32, (groups, TILE), 0)
+        channel = lax.broadcasted_iota(jnp.int32, (groups, TILE), 1)
+        return (group == j * groups_tile + channel // group_size).astype(F32)
+
+    def over_channels(table, chosen):
+        return jnp.dot(table, chosen, precision=HIGHEST, preferred_element_type=F32)
+
+    def as_line(table, chosen):
+        return jnp.sum(
+            jnp.where(own_lane, over_channels(table, chosen), 0.0), axis=0, keepdims=True
+        )
 
     @pl.loop(0, slices)
     def _(j):
         cols, lines = columns(j), group_rows(j)
-        taps[0:3, cols] = over_channels(kt_ref[lines, :].astype(F32))
-        taps[3:6, cols] = over_channels(vt_ref[lines, :].astype(F32))
-        rate_line = as_line(rates_ref[lines, :])
-        a_high, a_low = halves(jnp.where(member, as_line(res_ref[lines, :]), 0.0))
+        chosen = holds(j)
+        chosen_half = chosen.astype(BF16)
+        taps[0:3, cols] = jnp.dot(kt_ref[...], chosen_half, preferred_element_type=F32)
+        taps[3:6, cols] = jnp.dot(vt_ref[...], chosen_half, preferred_element_type=F32)
+        rate_line = as_line(rates_ref[...], chosen)
+        a_high, a_low = halves(jnp.where(member, as_line(res_ref[...], chosen), 0.0))
         weights = jnp.concatenate([a_high, a_high, a_low], axis=1)
         for table, filter_rows, lag in (
             (lag_up, filt, row_wide), (lag_down, turned, rows - 1.0 - row_wide)
@@ -244,9 +267,10 @@
 
     @pl.when(me < slices)
     def _():
-        rate_here = over_channels(rates_ref[group_rows(me), :])
+        chosen = holds(me)
+        rate_here = over_channels(rates_ref[...], chosen)
         fall = jnp.exp(-rate_here * float(rows))
-        scale = over_channels(res_ref[group_rows(me), :]) * jnp.exp(-rate_here)
+        scale = over_channels(res_ref[...], chosen) * jnp.exp(-rate_here)
 
         def step(i, carry):
             prefix[i] = carry * scale
@@ -261,6 +285,8 @@
         long_forward(j)
 
     row_acc[...] = jnp.zeros(row_acc.shape, F32)
+    load_q.wait()
+    load_og.wait()
 
     @pl.loop(0, slices)
     def _(i):
@@ -329,6 +355,9 @@
         own_b[j] = modal(lag_up, cols, mgrad[:, cols])
         scatter(2, own_b, gathered_b, j)
 
+    stores[0].start()
+    stores[1].start()
+
     def long_backward(j):
         cols = columns(j)
         mixed[:, cols] = toeplitz(filt, 0, j, mgrad, cols, tri_row <= tri_col)
@@ -339,9 +368,10 @@
 
     @pl.when(me < slices)
     def _():
-        rate_here = over_channels(rates_ref[group_rows(me), :])
+        chosen = holds(me)
+        rate_here = over_channels(rates_ref[...], chosen)
         fall = jnp.exp(-rate_here * float(rows))
-        scale = over_channels(res_ref[group_rows(me), :]) * jnp.exp(-rate_here)
+        scale = over_channels(res_ref[...], chosen) * jnp.exp(-rate_here)
 
         def step(i, carry):
             place = n - 1 - i
@@ -435,6 +465,10 @@
             shifted = (wide[0:16], wide[1:17], wide[2:18])
             target[rows - 16 : rows, cols] = mix(shifted, cols, 3 * which).astype(BF16)
 
+    stores[2].start()
+    stores[3].start()
+    by_group[...] = jnp.zeros(by_group.shape, F32)
+
     @pl.loop(0, slices)
     def _(j):
         @pl.when(j != me)
@@ -443,16 +477,19 @@
                 total.at[j], total.at[j], send_sem.at[5, 0], recv_sem.at[5, j], j
             ).wait_recv()
 
-        cols, lines = columns(j), group_rows(j)
+        cols = columns(j)
         here = total[j]
         skg_ref[0:1, cols] = here[0:1]
         gng_ref[0:1, cols] = here[1:2]
-        by_group = lax.dot_general(
-            member_wide, here, (((1,), (1,)), ((), ())),
+        by_group[...] += lax.dot_general(
+            here, holds(j), (((1,), (1,)), ((), ())),
             precision=HIGHEST, preferred_element_type=F32,
         )
-        ktg_ref[lines, :] = by_group[:, 2:5]
-        vtg_ref[lines, :] = by_group[:, 5:8]
+
+    ktg_ref[...] = by_group[2:5]
+    vtg_ref[...] = by_group[5:8]
+    for store in stores:
+        store.wait()
 
     @pl.when(me < n - 1)
     def _():
@@ -480,6 +517,18 @@
                 to_ctx(
                     total.at[me], total.at[me], send_sem.at[5, i], recv_sem.at[5, me], i
                 ).wait_send()
+
+
+def hand_over(*refs):
+    count = len(refs) // 2
+    sems = refs[-1]
+    copies = [
+        pltpu.make_async_copy(refs[i], refs[count + i], sems.at[i]) for i in range(count)
+    ]
+    for copy in copies:
+        copy.start()
+    for copy in copies:
+        copy.wait()
 
 
 def local(
@@ -496,14 +545,17 @@
     state = lambda count: pltpu.VMEM((count, group_size, TILE), F32)
     whole = lambda kind: pltpu.VMEM((rows, channels), kind)
     vmem = pl.BlockSpec(memory_space=pltpu.VMEM)
-    taps_shape = jax.ShapeDtypeStruct(key_taps.shape, F32)
+    anywhere = pl.BlockSpec(memory_space=pl.ANY)
+    taps_shape = jax.ShapeDtypeStruct((3, groups), F32)
     line_shape = jax.ShapeDtypeStruct((1, channels), F32)
-    *results, skip_grad, gain_grad = pl.pallas_call(
+    shapes = (wide,) * 4 + (taps_shape,) * 2 + (line_shape,) * 2
+    results = pl.pallas_call(
         functools.partial(body, n, n_ch, slices, float(channels * n_ch), group_size),
-        out_shape=(wide,) * 4 + (taps_shape,) * 2 + (line_shape,) * 2,
-        in_specs=[vmem] * 10,
-        out_specs=(vmem,) * 8,
+        out_shape=shapes,
+        in_specs=[anywhere] * 3 + [vmem] * 6 + [anywhere],
+        out_specs=(anywhere,) * 4 + (vmem,) * 4,
         scratch_shapes=[
+            *([whole(BF16)] * 8), pltpu.SemaphoreType.DMA((8,)), pltpu.VMEM((8, groups), F32),
             pltpu.VMEM((4, channels), F32), pltpu.VMEM((4, channels), F32),
             pltpu.VMEM((4, channels), F32), pltpu.VMEM((4, channels), F32),
             pltpu.VMEM((2, 16, channels), F32), pltpu.VMEM((2, 24, channels), F32),
@@ -526,10 +578,21 @@
         ),
         name="hyena",
     )(
-        query_proj, key_proj, value_proj, key_taps, value_taps, residues, decay_rates,
+        query_proj, key_proj, value_proj, key_taps.T, value_taps.T, residues.T, decay_rates.T,
         skip_weight.reshape(1, channels), norm_gain.reshape(1, channels), out_grad,
     )
-    return (*results, skip_grad.reshape(channels), gain_grad.reshape(channels))
+    results = pl.pallas_call(
+        hand_over,
+        out_shape=shapes,
+        in_specs=[anywhere] * len(shapes),
+        out_specs=(anywhere,) * len(shapes),
+        scratch_shapes=[pltpu.SemaphoreType.DMA((len(shapes),))],
+        name="hand_over",
+    )(*results)
+    return (
+        *results[:4], results[4].T, results[5].T,
+        results[6].reshape(channels), results[7].reshape(channels),
+    )
 
 
 def solution(mesh):

time: 86.7 us -> 205 us (2.36)
  Pallas kernels: 70.8 us -> 202 us
  local copies, waits for them, and re-layouts: 13.9 us -> 0 us
    pallas_call x0 -> x1, Pallas kernels: none -> 129 us  [local(): pl.pallas_call(hand_over, out_shape=shapes, in_specs=[anywhere] * len(sha...]
    unnamed x32 -> x0, local copies, waits for them, and re-layouts: 13.9 us -> none
    pallas_call x1, Pallas kernels: 70.8 us -> 73 us  [local(): pl.pallas_call(functools.partial(body, n, n_ch, slices, float(channels *...]
where the time goes in v3:
time: 205 us; the launch traced here: 203 us
  Pallas kernels  202 us (99%)
    pallas_call x1, Pallas kernels, local(): pl.pallas_call(hand_over, out_shape=shapes, in_specs=[anywhere] * len(sha...  129 us
    pallas_call x1, Pallas kernels, local(): pl.pallas_call(functools.partial(body, n, n_ch, slices, float(channels *...  73 us

profile of v3, /device:TPU:0, one launch (start us, length us, event | category | flops | bytes accessed | tf_op | source)
XLA Modules:
  0.0 203.1 jit_solution(366019267264063629)
XLA Ops:
  0.6 73.0 %hyena.1 = (bf16[128,4096]{1,0:T(8,128)(2,1)}, bf16[128,4096]{1,0:T(8,128)(2,1)}, bf16[128,4096]{1,0:T(8,128)(2,1)}, bf16[128,4096]{1,0:T(8,128)(2,1)}, f32[3,25...) custom-call(bf16[128,4096]{1,0:T(8,128)(2,1)} %q_hbm.1, bf16[128,4096]{1,0:T(8,128)(2,1)} %k_hbm.1, ...), custom_call_target="tpu_custom_call" | custom-call | tf_op jit(solution)/shard_map/hyena/pallas_call | solution.py:552
  73.7 129.5 %hand_over.1 = (bf16[128,4096]{1,0:T(8,128)(2,1)}, bf16[128,4096]{1,0:T(8,128)(2,1)}, bf16[128,4096]{1,0:T(8,128)(2,1)}, bf16[128,4096]{1,0:T(8,128)(2,1)}, f32[...) custom-call(bf16[128,4096]{1,0:T(8,128)(2,1)} %get-tuple-element.24.refs_0_, ...), custom_call_target="tpu_custom_call" | custom-call | tf_op jit(solution)/shard_map/hand_over/pallas_call | solution.py:584

commit v4 on v3

--- a/solution.py
+++ b/solution.py
@@ -105,10 +105,17 @@
     def group_rows(j):
         return pl.ds(pl.multiple_of(j * groups_tile, groups_tile), groups_tile)
 
+    gap = (
+        lax.broadcasted_iota(jnp.int32, (groups, TILE), 0)
+        - lax.broadcasted_iota(jnp.int32, (groups, TILE), 1) // group_size
+    )
+    gap_turned = (
+        lax.broadcasted_iota(jnp.int32, (TILE, groups), 1)
+        - lax.broadcasted_iota(jnp.int32, (TILE, groups), 0) // group_size
+    )
+
     def holds(j):
-        group = lax.broadcasted_iota(jnp.int32, (groups, TILE), 0)
-        channel = lax.broadcasted_iota(jnp.int32, (groups, TILE), 1)
-        return (group == j * groups_tile + channel // group_size).astype(F32)
+        return (gap == j * groups_tile).astype(F32)
 
     def over_channels(table, chosen):
         return jnp.dot(table, chosen, precision=HIGHEST, preferred_element_type=F32)
@@ -481,8 +488,8 @@
         here = total[j]
         skg_ref[0:1, cols] = here[0:1]
         gng_ref[0:1, cols] = here[1:2]
-        by_group[...] += lax.dot_general(
-            here, holds(j), (((1,), (1,)), ((), ())),
+        by_group[...] += jnp.dot(
+            here, (gap_turned == j * groups_tile).astype(F32),
             precision=HIGHEST, preferred_element_type=F32,
         )
 
@@ -519,16 +526,22 @@
                 ).wait_send()
 
 
-def hand_over(*refs):
-    count = len(refs) // 2
+def hand_over(count, *refs):
+    sources, targets, staged = refs[:count], refs[count : 2 * count], refs[2 * count : 3 * count]
     sems = refs[-1]
-    copies = [
-        pltpu.make_async_copy(refs[i], refs[count + i], sems.at[i]) for i in range(count)
+    loads = [
+        pltpu.make_async_copy(sources[i], staged[i], sems.at[i]) for i in range(count)
     ]
-    for copy in copies:
-        copy.start()
-    for copy in copies:
-        copy.wait()
+    stores = [
+        pltpu.make_async_copy(staged[i], targets[i], sems.at[count + i]) for i in range(count)
+    ]
+    for load in loads:
+        load.start()
+    for load, store in zip(loads, stores):
+        load.wait()
+        store.start()
+    for store in stores:
+        store.wait()
 
 
 def local(
@@ -582,11 +595,14 @@
         skip_weight.reshape(1, channels), norm_gain.reshape(1, channels), out_grad,
     )
     results = pl.pallas_call(
-        hand_over,
+        functools.partial(hand_over, len(shapes)),
         out_shape=shapes,
         in_specs=[anywhere] * len(shapes),
         out_specs=(anywhere,) * len(shapes),
-        scratch_shapes=[pltpu.SemaphoreType.DMA((len(shapes),))],
+        scratch_shapes=[
+            *(pltpu.VMEM(shape.shape, shape.dtype) for shape in shapes),
+            pltpu.SemaphoreType.DMA((2 * len(shapes),)),
+        ],
         name="hand_over",
     )(*results)
     return (

time: 205 us -> 76.7 us (0.37)
  Pallas kernels: 202 us -> 74.9 us
    pallas_call x1, Pallas kernels: 129 us -> 3.38 us  [local(): pl.pallas_call(functools.partial(hand_over, len(shapes)), out_shape=shape...]
where the time goes in v4:
time: 76.7 us; the launch traced here: 75.5 us
  Pallas kernels  74.9 us (98%)
    pallas_call x1, Pallas kernels, local(): pl.pallas_call(functools.partial(body, n, n_ch, slices, float(channels *...  71.5 us
    pallas_call x1, Pallas kernels, local(): pl.pallas_call(functools.partial(hand_over, len(shapes)), out_shape=shape...  3.38 us

profile of v4, /device:TPU:0, one launch (start us, length us, event | category | flops | bytes accessed | tf_op | source)
XLA Modules:
  0.0 75.5 jit_solution(1871742776788492956)
XLA Ops:
  0.6 71.5 %hyena.1 = (bf16[128,4096]{1,0:T(8,128)(2,1)}, bf16[128,4096]{1,0:T(8,128)(2,1)}, bf16[128,4096]{1,0:T(8,128)(2,1)}, bf16[128,4096]{1,0:T(8,128)(2,1)}, f32[3,25...) custom-call(bf16[128,4096]{1,0:T(8,128)(2,1)} %q_hbm.1, bf16[128,4096]{1,0:T(8,128)(2,1)} %k_hbm.1, ...), custom_call_target="tpu_custom_call" | custom-call | tf_op jit(solution)/shard_map/hyena/pallas_call | solution.py:565
  72.2 3.4 %hand_over.1 = (bf16[128,4096]{1,0:T(8,128)(2,1)}, bf16[128,4096]{1,0:T(8,128)(2,1)}, bf16[128,4096]{1,0:T(8,128)(2,1)}, bf16[128,4096]{1,0:T(8,128)(2,1)}, f32[...) custom-call(bf16[128,4096]{1,0:T(8,128)(2,1)} %get-tuple-element.24.refs_0_, ...), custom_call_target="tpu_custom_call" | custom-call | tf_op jit(solution)/shard_map/hand_over/pallas_call | solution.py:597
